TPU v7x, 128 devices: a whole 4x4x4 slice. The times are simulated.
128 devices in a mesh: grp: 4 (over y), row: 32 (over x, z, core).
Axes of the slice: x: 4, y: 4, z: 4, core: 2. Of those that a mesh axis runs over, the one named last changes fastest.
Arguments:
- b_tensor: bfloat16 [9984, 8, 768], P(None, 'grp', 'row'), may hold values from -0.21875 to 0.21875
- aux_counts: int32 [4], replicated, may hold values from 1 to 2, as said below
Outputs:
- exchange_matrix: float32 [9984, 9984], P('row', 'grp')
Inputs may be any that keep to these rules, and one draw needn't show every extreme that they name: `aux_counts`: some group has all 2 slots live.
All inputs are finite; a program needn't handle non-finite values.
Results may differ from a plain program's by a relative error of at most 0.0003.
Values may be sent and summed in bfloat16 or wider, within the bound.
No kernel may reach another device: no remote copies, remote signals or barrier semaphores. Data moves between devices by JAX's collectives and lax.ppermute only.
A program may use at most 128 MiB of HBM per device.

v0:
```python
import jax
import jax.numpy as jnp
from jax import lax
from jax.experimental import pallas as pl
from jax.experimental.pallas import tpu as pltpu
from jax.sharding import Mesh, PartitionSpec as P


SIDE = 4
CORES = 2
PLANE = SIDE * SIDE
SOURCES = CORES * SIDE
WIDE = 1280
VMEM = pl.BlockSpec(memory_space=pltpu.VMEM)
SMEM = pl.BlockSpec(memory_space=pltpu.SMEM)


def along_y(block, step):
    return lax.ppermute(block, "y", [(i, (i + step) % SIDE) for i in range(SIDE)])


def swap_cores(block):
    return lax.ppermute(block, "core", [(0, 1), (1, 0)])


def along_plane(block, order, step):
    route = []
    for x in range(SIDE):
        for z in range(SIDE):
            for core in range(CORES):
                to = ((x + step) % SIDE, z) if core == order else (x, (z + step) % SIDE)
                route.append(((x * SIDE + z) * CORES + core, (to[0] * SIDE + to[1]) * CORES + core))
    return lax.ppermute(block, ("x", "z", "core"), route)


def join(blocks):
    def kernel(*refs):
        at = 0
        for ref in refs[:-1]:
            refs[-1][at : at + ref.shape[0]] = ref[...]
            at += ref.shape[0]

    total = sum(block.shape[0] for block in blocks)
    joined = jax.ShapeDtypeStruct((total, *blocks[0].shape[1:]), blocks[0].dtype)
    size = joined.size * joined.dtype.itemsize
    return pl.pallas_call(
        kernel,
        out_shape=joined,
        in_specs=[VMEM] * len(blocks),
        out_specs=VMEM,
        compiler_params=pltpu.CompilerParams(vmem_limit_bytes=4 * size),
        cost_estimate=pl.CostEstimate(flops=0, bytes_accessed=2 * size, transcendentals=0),
        name="join",
    )(*blocks)


def pack_kernel(count_ref, terms_ref, *refs):
    window_refs, rows_ref, windows = refs[:SOURCES], refs[-2], refs[-1]
    slots, orbitals, basis = terms_ref.shape
    columns = basis // SIDE
    chip_rows = rows_ref.shape[2]
    y, core = lax.axis_index("y"), lax.axis_index("core")
    for s in range(slots):
        live = s < count_ref[y]
        at = pl.ds(s * orbitals, orbitals)
        for p in range(SIDE):
            for q in range(CORES):
                start = p * columns + q * WIDE
                width = min(WIDE, basis - start)
                block = terms_ref[s, :, start : start + width]
                windows[p * CORES + q, at, :width] = jnp.where(live, block, jnp.zeros_like(block))
                if width < WIDE:
                    windows[p * CORES + q, at, width:] = jnp.zeros((orbitals, WIDE - width), block.dtype)
        for i in range(PLANE):
            block = terms_ref[s, :, i * chip_rows : (i + 1) * chip_rows]
            rows_ref[i, at, :] = jnp.where(live, block, jnp.zeros_like(block))
    for dcore in range(CORES):
        for dy in range(SIDE):
            to = lax.rem(y + dy, SIDE) * CORES + lax.rem(core + dcore, CORES)
            window_refs[dcore * SIDE + dy][...] = windows[to]


def pack(counts, terms):
    slots, orbitals, basis = terms.shape
    depth = slots * orbitals
    window = jax.ShapeDtypeStruct((depth, WIDE), terms.dtype)
    chip_rows = jax.ShapeDtypeStruct((PLANE, depth, basis // PLANE), terms.dtype)
    *windows, rows = pl.pallas_call(
        pack_kernel,
        out_shape=(window,) * SOURCES + (chip_rows,),
        in_specs=[SMEM, VMEM],
        out_specs=(VMEM,) * (SOURCES + 1),
        scratch_shapes=[pltpu.VMEM((SOURCES, depth, WIDE), terms.dtype)],
        compiler_params=pltpu.CompilerParams(vmem_limit_bytes=10 << 20),
        name="pack",
    )(counts, terms)
    return windows, rows


def exchanged(windows):
    from_offset = {}
    for dcore in range(CORES):
        for dy in (2, 1, 3, 0):
            block = windows[dcore * SIDE + dy]
            if dy or dcore:
                route = [
                    (y * CORES + core, (y + dy) % SIDE * CORES + (core + dcore) % CORES)
                    for y in range(SIDE)
                    for core in range(CORES)
                ]
                block = lax.ppermute(block, ("y", "core"), route)
            from_offset[dcore, -dy % SIDE] = block
    return join([from_offset[dcore, dy] for dcore in range(CORES) for dy in range(SIDE)])


def gathered(own):
    depth = own.shape[0]
    cut = depth // 2
    before, after = along_plane(own, 0, 1), along_plane(own, 0, -1)
    near = join([before, after])
    own_sides = along_plane(own, 1, 1), along_plane(own, 1, -1)
    near_sides = along_plane(near, 1, 1), along_plane(near, 1, -1)
    far = along_plane(before, 0, 1)
    far_sides = along_plane(far, 1, 1), along_plane(far, 1, -1)
    own_opposite = along_plane(own_sides[0], 1, 1)
    near_opposite = along_plane(near_sides[0][:cut], 1, 1), along_plane(near_sides[1][cut:], 1, -1)
    far_opposite = along_plane(far_sides[1], 1, -1)

    def at(v, *us):
        return tuple((u, v) for u in us)

    parts = [(at(0, 0), 0, own), (at(0, -1, 1), 0, near), (at(0, 2), 0, far)]
    parts += [(at(v, 0), 0, block) for v, block in zip((-1, 1), own_sides)]
    parts += [(at(v, -1, 1), 0, block) for v, block in zip((-1, 1), near_sides)]
    parts += [(at(2, 0), 0, own_opposite)]
    parts += [(at(v, 2), 0, block) for v, block in zip((-1, 1), far_sides)]
    parts += [(at(2, -1, 1), 0, near_opposite[0]), (at(2, -1, 1), SOURCES // 2, near_opposite[1])]
    parts += [(at(2, 2), 0, far_opposite)]
    return parts


def arrange_kernel(layout, rows_ref, rest_ref, other_rows_ref, other_rest_ref, *out_refs):
    depth = rows_ref.shape[1]
    x, z, core = (lax.axis_index(name) for name in ("x", "z", "core"))
    for blocks, out_ref in zip(layout, out_refs):
        for i, (u, v, source) in enumerate(blocks):
            dx, dz = jnp.where(core == 0, u, v), jnp.where(core == 0, v, u)
            chip = lax.rem(x + dx + SIDE, SIDE) * SIDE + lax.rem(z + dz + SIDE, SIDE)
            dcore, dy = divmod(source, SIDE)
            if dy == 0:
                block = (rows_ref, other_rows_ref)[dcore][chip]
            else:
                block = (rest_ref, other_rest_ref)[dcore][(dy - 1) * PLANE + chip]
            out_ref[i * depth : (i + 1) * depth, :] = block


def arrange(layout, rows, rest, other_rows, other_rest):
    depth, chip_rows = rows.shape[1:]
    return pl.pallas_call(
        lambda *refs: arrange_kernel(layout, *refs),
        out_shape=tuple(jax.ShapeDtypeStruct((len(blocks) * depth, chip_rows), rows.dtype) for blocks in layout),
        in_specs=[VMEM] * 4,
        out_specs=(VMEM,) * len(layout),
        compiler_params=pltpu.CompilerParams(vmem_limit_bytes=20 << 20),
        name="arrange",
    )(rows, rest, other_rows, other_rest)


def assemble_kernel(tile_ref, got_ref, out_ref):
    rest = out_ref.shape[1] - WIDE
    for core in range(CORES):

        @pl.when(lax.axis_index("core") == core)
        def _():
            first, last = (tile_ref.at[core], got_ref) if core == 0 else (got_ref, tile_ref.at[core])
            out_ref[:, :WIDE] = first[...]
            out_ref[:, WIDE:] = last[:, :rest]


def assemble(tile, got, columns):
    return pl.pallas_call(
        assemble_kernel,
        out_shape=jax.ShapeDtypeStruct((got.shape[0], columns), got.dtype),
        in_specs=[VMEM, VMEM],
        out_specs=VMEM,
        compiler_params=pltpu.CompilerParams(vmem_limit_bytes=20 << 20),
        name="assemble",
    )(tile, got)


def body(b_tensor, aux_counts):
    basis = b_tensor.shape[0]
    core = lax.axis_index("core")
    windows, rows = pack(aux_counts, b_tensor.transpose(1, 2, 0))
    chip_rows = rows.shape[2]

    columns = exchanged(windows)
    rows = lax.all_to_all(rows, ("x", "z"), 0, 0, tiled=True)
    parts = gathered(columns)

    left, right = along_y(rows, 1), along_y(rows, -1)
    half = PLANE // 2
    far = along_y(left[:half], 1), along_y(right[half:], -1)
    rest = join([right, *far, left])
    other_rows = swap_cores(rows)
    other_rest = swap_cores(rest)

    layout = []
    for offsets, skipped, block in parts:
        blocks = [(u, v, source) for u, v in offsets for source in range(SOURCES)]
        layout.append(blocks[skipped : skipped + block.shape[0] // rows.shape[1]])
    weights = arrange(layout, rows, rest, other_rows, other_rest)

    tile = None
    for (_, _, block), weight in zip(parts, weights):
        product = lax.dot_general(weight, block, (((0,), (0,)), ((), ())), preferred_element_type=jnp.float32)
        tile = lax.optimization_barrier(product if tile is None else tile + product)

    tile = tile.reshape(CORES, chip_rows // CORES, WIDE)
    got = swap_cores(lax.dynamic_index_in_dim(tile, 1 - core, 0, keepdims=False))
    return assemble(tile, got, basis // SIDE)


def solution(mesh):
    fine = Mesh(mesh.devices.reshape(SIDE, SIDE, SIDE, CORES), ("y", "x", "z", "core"))
    return jax.shard_map(
        body,
        mesh=fine,
        in_specs=(P(None, "y", ("x", "z", "core")), P()),
        out_specs=P(("x", "z", "core"), "y"),
        check_vma=False,
    )
```

profile of v0, /device:TPU:1, one launch (start us, length us, event | category | flops | bytes accessed | tf_op | source)
XLA Modules:
  0.0 197.1 jit_solution(16447629656757655697)
XLA Ops:
  3.0 23.6 %all_to_all.5.refs_0_ = bf16[16,48,624]{2,1,0:T(8,128)(2,1)} all-to-all(bf16[16,48,624]{2,1,0:T(8,128)(2,1)S(1)} %get-tuple-element.27), channel_id=1, replica_groups=mesh['y'=4,'x'=4,'z'=4,'core'=2] {'x','z'}, dimensions={0} | all-to-all | bytes 1916928 | tf_op jit(solution)/shard_map/all_to_all | solution.py:198
  31.8 20.1 %collective-permute-done.6.refs_1_ = bf16[48,1280]{1,0:T(8,128)(2,1)S(1)} collective-permute-done((bf16[48,1280]{1,0:T(8,128)(2,1)S(1)}, bf16[48,1280]{1,0:T(8,128)(2,1)S(1)}, u32[]{:S(2)}, u32[]{:S(2)}) %collective-permute-start.6) | collective-permute-done | bytes 122912 | tf_op jit(solution)/shard_map/ppermute | solution.py:111
  51.9 4.3 %collective-permute-start.9 = (bf16[48,1280]{1,0:T(8,128)(2,1)S(1)}, bf16[48,1280]{1,0:T(8,128)(2,1)S(1)}, u32[]{:S(2)}, u32[]{:S(2)}) collective-permute-start(bf16[48,1280]{1,0:T(8,128)(2,1)S(1)} %get-tuple-element.33), channel_id=1, source_target_pairs={{0,1},{1,0},{32,33},{33,32},{64,65},{65,64},{96,97},{97,96},{2,3},... | collective-permute-start | bytes 368648 | tf_op jit(solution)/shard_map/ppermute | solution.py:111
  56.2 3.9 %collective-permute-start.10 = (bf16[48,1280]{1,0:T(8,128)(2,1)S(1)}, bf16[48,1280]{1,0:T(8,128)(2,1)S(1)}, u32[]{:S(2)}, u32[]{:S(2)}) collective-permute-start(bf16[48,1280]{1,0:T(8,128)(2,1)S(1)} %get-tuple-element.34), channel_id=1, source_target_pairs={{0,97},{1,96},{32,1},{33,0},{64,33},{65,32},{96,65},{97,64},{2,99}... | collective-permute-start | bytes 368648 | tf_op jit(solution)/shard_map/ppermute | solution.py:111
  61.1 4.0 %collective-permute-done.10.refs_5_ = bf16[48,1280]{1,0:T(8,128)(2,1)S(1)} collective-permute-done((bf16[48,1280]{1,0:T(8,128)(2,1)S(1)}, bf16[48,1280]{1,0:T(8,128)(2,1)S(1)}, u32[]{:S(2)}, u32[]{:S(2)}) %collective-permute-start.10) | collective-permute-done | bytes 122912 | tf_op jit(solution)/shard_map/ppermute | solution.py:111
  65.1 2.1 %collective-permute-done.11.refs_6_ = bf16[48,1280]{1,0:T(8,128)(2,1)S(1)} collective-permute-done((bf16[48,1280]{1,0:T(8,128)(2,1)S(1)}, bf16[48,1280]{1,0:T(8,128)(2,1)S(1)}, u32[]{:S(2)}, u32[]{:S(2)}) %collective-permute-start.11) | collective-permute-done | bytes 122912 | tf_op jit(solution)/shard_map/ppermute | solution.py:111
  67.2 2.5 %collective-permute-done.12.refs_7_ = bf16[48,1280]{1,0:T(8,128)(2,1)S(1)} collective-permute-done((bf16[48,1280]{1,0:T(8,128)(2,1)S(1)}, bf16[48,1280]{1,0:T(8,128)(2,1)S(1)}, u32[]{:S(2)}, u32[]{:S(2)}) %collective-permute-start.12) | collective-permute-done | bytes 122912 | tf_op jit(solution)/shard_map/ppermute | solution.py:111
  71.3 2.1 %collective-permute-start.14 = (bf16[384,1280]{1,0:T(8,128)(2,1)}, bf16[384,1280]{1,0:T(8,128)(2,1)S(1)}, u32[]{:S(2)}, u32[]{:S(2)}) collective-permute-start(bf16[384,1280]{1,0:T(8,128)(2,1)} %join.4), channel_id=1, source_target_pairs={{0,24},{1,7},{2,26},{3,1},{4,28},{5,3},{6,30},{7,5},{8,0},{9,15},{... | collective-permute-start | bytes 2949128 | tf_op jit(solution)/shard_map/ppermute | solution.py:33
  73.7 2.7 %collective-permute-start.3 = (bf16[8,48,624]{2,1,0:T(8,128)(2,1)S(1)}, bf16[8,48,624]{2,1,0:T(8,128)(2,1)S(1)}, u32[]{:S(2)}, u32[]{:S(2)}) collective-permute-start(bf16[8,48,624]{2,1,0:T(8,128)(2,1)S(1)} %slice.17), channel_id=1, source_target_pairs={{0,96},{32,0},{64,32},{96,64},{1,97},{33,1},{65,33},{97,65},{2,98}... | collective-permute-start | bytes 1437704 | tf_op jit(solution)/shard_map/ppermute | solution.py:19
  76.4 9.2 %collective-permute-done.13.refs_0_ = bf16[384,1280]{1,0:T(8,128)(2,1)} collective-permute-done((bf16[384,1280]{1,0:T(8,128)(2,1)}, bf16[384,1280]{1,0:T(8,128)(2,1)}, u32[]{:S(2)}, u32[]{:S(2)}) %collective-permute-start.13) | collective-permute-done | bytes 983072 | tf_op jit(solution)/shard_map/ppermute | solution.py:33
  85.6 2.6 %join.5 = bf16[768,1280]{1,0:T(8,128)(2,1)} custom-call(bf16[384,1280]{1,0:T(8,128)(2,1)} %collective-permute-done.13.refs_0_, bf16[384,1280]{1,0:T(8,128)(2,1)S(1)} %collective-permute-done.14.refs_1_), custom_call_target="tpu_custom_call" | custom-call | bytes 3932160 | tf_op jit(solution)/shard_map/join/pallas_call | solution.py:46
  88.4 2.3 %collective-permute-start.5 = (bf16[48,48,624]{2,1,0:T(8,128)(2,1)S(1)}, bf16[48,48,624]{2,1,0:T(8,128)(2,1)}, u32[]{:S(2)}, u32[]{:S(2)}) collective-permute-start(bf16[48,48,624]{2,1,0:T(8,128)(2,1)S(1)} %join.3.refs_1_), channel_id=1, source_target_pairs={{0,1},{1,0},{2,3},{3,2},{4,5},{5,4},{6,7},{7,6},{8,9},{9,8},{10,11... | collective-permute-start | bytes 8626184 | tf_op jit(solution)/shard_map/ppermute | solution.py:23
  90.7 2.8 %collective-permute-start.19 = (bf16[768,1280]{1,0:T(8,128)(2,1)}, bf16[768,1280]{1,0:T(8,128)(2,1)}, u32[]{:S(2)}, u32[]{:S(2)}) collective-permute-start(bf16[768,1280]{1,0:T(8,128)(2,1)} %join.5), channel_id=1, source_target_pairs={{0,6},{1,25},{2,0},{3,27},{4,2},{5,29},{6,4},{7,31},{8,14},{9,1},{... | collective-permute-start | bytes 5898248 | tf_op jit(solution)/shard_map/ppermute | solution.py:33
  93.6 30.4 %collective-permute-done.18 = bf16[768,1280]{1,0:T(8,128)(2,1)} collective-permute-done((bf16[768,1280]{1,0:T(8,128)(2,1)}, bf16[768,1280]{1,0:T(8,128)(2,1)}, u32[]{:S(2)}, u32[]{:S(2)}) %collective-permute-start.18) | collective-permute-done | bytes 1966112 | tf_op jit(solution)/shard_map/ppermute | solution.py:33
  124.0 2.2 %collective-permute-start.4 = (bf16[16,48,624]{2,1,0:T(8,128)(2,1)}, bf16[16,48,624]{2,1,0:T(8,128)(2,1)}, u32[]{:S(2)}, u32[]{:S(2)}) collective-permute-start(bf16[16,48,624]{2,1,0:T(8,128)(2,1)} %all_to_all.5.refs_0_), channel_id=1, source_target_pairs={{0,1},{1,0},{2,3},{3,2},{4,5},{5,4},{6,7},{7,6},{8,9},{9,8},{10,11... | collective-permute-start | bytes 2875400 | tf_op jit(solution)/shard_map/ppermute | solution.py:23
  127.3 7.2 %collective-permute-done.16 = bf16[384,1280]{1,0:T(8,128)(2,1)} collective-permute-done((bf16[384,1280]{1,0:T(8,128)(2,1)}, bf16[384,1280]{1,0:T(8,128)(2,1)}, u32[]{:S(2)}, u32[]{:S(2)}) %collective-permute-start.16) | collective-permute-done | bytes 983072 | tf_op jit(solution)/shard_map/ppermute | solution.py:33
  134.5 1.5 collective-permute-start.20
  136.1 1.5 slice.19
  137.6 2.7 %collective-permute-start.22 = (bf16[384,1280]{1,0:T(8,128)(2,1)}, bf16[384,1280]{1,0:T(8,128)(2,1)S(1)}, u32[]{:S(2)}, u32[]{:S(2)}) collective-permute-start(bf16[384,1280]{1,0:T(8,128)(2,1)} %collective-permute-done.15), channel_id=1, source_target_pairs={{0,6},{1,25},{2,0},{3,27},{4,2},{5,29},{6,4},{7,31},{8,14},{9,1},{... | collective-permute-start | bytes 2949128 | tf_op jit(solution)/shard_map/ppermute | solution.py:33
  140.2 3.0 %arrange.1 = (bf16[384,624]{1,0:T(8,128)(2,1)S(1)}, bf16[768,624]{1,0:T(8,128)(2,1)S(1)}, bf16[384,624]{1,0:T(8,128)(2,1)S(1)}, bf16[384,624]{1,0:T(8,128)(2,1)S...) custom-call(bf16[16,48,624]{2,1,0:T(8,128)(2,1)} %all_to_all.5.refs_, ...), custom_call_target="tpu_custom_call" | custom-call | tf_op jit(solution)/shard_map/arrange/pallas_call | solution.py:159
  143.2 2.2 %fusion = f32[624,1280]{1,0:T(8,128)S(1)} fusion(bf16[384,624]{1,0:T(8,128)(2,1)S(1)} %get-tuple-element.28, bf16[384,1280]{1,0:T(8,128)(2,1)} %join.4), kind=kOutput, calls=%fused_computation.5 | convolution fusion | flops 613416960 | bytes 4657152 | tf_op jit(solution)/shard_map/dot_general | solution.py:216
  145.5 3.0 %fusion.1 = f32[624,1280]{1,0:T(8,128)S(1)} fusion(bf16[768,624]{1,0:T(8,128)(2,1)S(1)} %get-tuple-element.37, bf16[768,1280]{1,0:T(8,128)(2,1)} %join.5), kind=kOutput, calls=%fused_computation.6 | convolution fusion | flops 1226833920 | bytes 6119424 | tf_op jit(solution)/shard_map/dot_general | solution.py:216
  148.9 2.2 %convolution_add_fusion.3 = f32[624,1280]{1,0:T(8,128)S(1)} fusion(f32[624,1280]{1,0:T(8,128)S(1)} %add.41, bf16[384,624]{1,0:T(8,128)(2,1)S(1)} %get-tuple-element.38, bf16[384,1280]{1,0:T(8,128)(2,1)} %collective-permute-done.15), kind=kOutput, calls=%fused_computation.3 | convolution fusion | flops 614215680 | bytes 7852032 | tf_op jit(solution)/shard_map/dot_general | solution.py:216
  151.1 2.2 %fusion.2 = f32[624,1280]{1,0:T(8,128)S(1)} fusion(bf16[384,624]{1,0:T(8,128)(2,1)S(1)} %get-tuple-element.39, bf16[384,1280]{1,0:T(8,128)(2,1)} %collective-permute-done.16), kind=kOutput, calls=%fused_computation.7 | convolution fusion | flops 613416960 | bytes 4657152 | tf_op jit(solution)/shard_map/dot_general | solution.py:216
  153.7 3.0 %fusion.4 = f32[624,1280]{1,0:T(8,128)S(1)} fusion(bf16[768,624]{1,0:T(8,128)(2,1)S(1)} %get-tuple-element.41, bf16[768,1280]{1,0:T(8,128)(2,1)} %collective-permute-done.18), kind=kOutput, calls=%fused_computation.9 | convolution fusion | flops 1226833920 | bytes 6119424 | tf_op jit(solution)/shard_map/dot_general | solution.py:216
  156.7 2.7 %collective-permute-start.24 = (bf16[576,1280]{1,0:T(8,128)(2,1)S(1)}, bf16[576,1280]{1,0:T(8,128)(2,1)S(1)}, u32[]{:S(2)}, u32[]{:S(2)}) collective-permute-start(bf16[576,1280]{1,0:T(8,128)(2,1)S(1)} %slice.19), channel_id=1, source_target_pairs={{0,6},{1,25},{2,0},{3,27},{4,2},{5,29},{6,4},{7,31},{8,14},{9,1},{... | collective-permute-start | bytes 4423688 | tf_op jit(solution)/shard_map/ppermute | solution.py:33
  161.6 3.0 %fusion.5 = f32[624,1280]{1,0:T(8,128)S(1)} fusion(bf16[768,624]{1,0:T(8,128)(2,1)S(1)} %get-tuple-element.42, bf16[768,1280]{1,0:T(8,128)(2,1)} %collective-permute-done.19), kind=kOutput, calls=%fused_computation.10 | convolution fusion | flops 1226833920 | bytes 6119424 | tf_op jit(solution)/shard_map/dot_general | solution.py:216
  169.6 6.2 %collective-permute-done.24 = bf16[576,1280]{1,0:T(8,128)(2,1)S(1)} collective-permute-done((bf16[576,1280]{1,0:T(8,128)(2,1)S(1)}, bf16[576,1280]{1,0:T(8,128)(2,1)S(1)}, u32[]{:S(2)}, u32[]{:S(2)}) %collective-permute-start.24) | collective-permute-done | bytes 1474592 | tf_op jit(solution)/shard_map/ppermute | solution.py:33
  177.6 8.7 %collective-permute-done.25 = bf16[384,1280]{1,0:T(8,128)(2,1)S(1)} collective-permute-done((bf16[384,1280]{1,0:T(8,128)(2,1)S(1)}, bf16[384,1280]{1,0:T(8,128)(2,1)S(1)}, u32[]{:S(2)}, u32[]{:S(2)}) %collective-permute-start.25) | collective-permute-done | bytes 983072 | tf_op jit(solution)/shard_map/ppermute | solution.py:33
  187.5 4.6 %collective-permute-start.26 = (f32[312,1280]{1,0:T(8,128)S(1)}, f32[312,1280]{1,0:T(8,128)S(1)}, u32[]{:S(2)}, u32[]{:S(2)}) collective-permute-start(f32[312,1280]{1,0:T(8,128)S(1)} %dynamic-slice_bitcast_fusion), channel_id=1, source_target_pairs={{0,1},{1,0},{2,3},{3,2},{4,5},{5,4},{6,7},{7,6},{8,9},{9,8},{10,11... | collective-permute-start | bytes 4792328 | tf_op jit(solution)/shard_map/ppermute | solution.py:23
  192.1 3.1 %collective-permute-done.26.got_ref = f32[312,1280]{1,0:T(8,128)S(1)} collective-permute-done((f32[312,1280]{1,0:T(8,128)S(1)}, f32[312,1280]{1,0:T(8,128)S(1)}, u32[]{:S(2)}, u32[]{:S(2)}) %collective-permute-start.26) | collective-permute-done | bytes 1597472 | tf_op jit(solution)/shard_map/ppermute | solution.py:23
  195.2 1.9 assemble.1
  (59 shorter events, 23.4 us)
Async XLA Ops:
  0.0 1.2 copy-start
  1.2 0.7 copy-start.1
  26.6 46.9 %collective-permute-start.1 = (bf16[16,48,624]{2,1,0:T(8,128)(2,1)}, bf16[16,48,624]{2,1,0:T(8,128)(2,1)S(1)}, u32[]{:S(2)}, u32[]{:S(2)}) collective-permute-start(bf16[16,48,624]{2,1,0:T(8,128)(2,1)} %all_to_all.5.refs_0_), channel_id=1, source_target_pairs={{0,32},{32,64},{64,96},{96,0},{1,33},{33,65},{65,97},{97,1},{2,34}... | collective-permute-start | bytes 2875400 | tf_op jit(solution)/shard_map/ppermute | solution.py:19
  27.9 45.7 %collective-permute-start = (bf16[16,48,624]{2,1,0:T(8,128)(2,1)}, bf16[16,48,624]{2,1,0:T(8,128)(2,1)S(1)}, u32[]{:S(2)}, u32[]{:S(2)}) collective-permute-start(bf16[16,48,624]{2,1,0:T(8,128)(2,1)} %all_to_all.5.refs_0_), channel_id=1, source_target_pairs={{0,96},{32,0},{64,32},{96,64},{1,97},{33,1},{65,33},{97,65},{2,98}... | collective-permute-start | bytes 2875400 | tf_op jit(solution)/shard_map/ppermute | solution.py:19
  29.3 22.6 %collective-permute-start.6 = (bf16[48,1280]{1,0:T(8,128)(2,1)S(1)}, bf16[48,1280]{1,0:T(8,128)(2,1)S(1)}, u32[]{:S(2)}, u32[]{:S(2)}) collective-permute-start(bf16[48,1280]{1,0:T(8,128)(2,1)S(1)} %get-tuple-element.30), channel_id=1, source_target_pairs={{0,96},{1,97},{32,0},{33,1},{64,32},{65,33},{96,64},{97,65},{2,98}... | collective-permute-start | bytes 368648 | tf_op jit(solution)/shard_map/ppermute | solution.py:111
  30.8 25.4 %collective-permute-start.7 = (bf16[48,1280]{1,0:T(8,128)(2,1)S(1)}, bf16[48,1280]{1,0:T(8,128)(2,1)S(1)}, u32[]{:S(2)}, u32[]{:S(2)}) collective-permute-start(bf16[48,1280]{1,0:T(8,128)(2,1)S(1)} %get-tuple-element.31), channel_id=1, source_target_pairs={{0,64},{1,65},{32,96},{33,97},{64,0},{65,1},{96,32},{97,33},{2,66}... | collective-permute-start | bytes 368648 | tf_op jit(solution)/shard_map/ppermute | solution.py:111
  31.1 28.9 %collective-permute-start.8 = (bf16[48,1280]{1,0:T(8,128)(2,1)S(1)}, bf16[48,1280]{1,0:T(8,128)(2,1)S(1)}, u32[]{:S(2)}, u32[]{:S(2)}) collective-permute-start(bf16[48,1280]{1,0:T(8,128)(2,1)S(1)} %get-tuple-element.32), channel_id=1, source_target_pairs={{0,32},{1,33},{32,64},{33,65},{64,96},{65,97},{96,0},{97,1},{2,34}... | collective-permute-start | bytes 368648 | tf_op jit(solution)/shard_map/ppermute | solution.py:111
  51.9 8.1 %collective-permute-start.9 = (bf16[48,1280]{1,0:T(8,128)(2,1)S(1)}, bf16[48,1280]{1,0:T(8,128)(2,1)S(1)}, u32[]{:S(2)}, u32[]{:S(2)}) collective-permute-start(bf16[48,1280]{1,0:T(8,128)(2,1)S(1)} %get-tuple-element.33), channel_id=1, source_target_pairs={{0,1},{1,0},{32,33},{33,32},{64,65},{65,64},{96,97},{97,96},{2,3},... | collective-permute-start | bytes 368648 | tf_op jit(solution)/shard_map/ppermute | solution.py:111
  56.2 8.9 %collective-permute-start.10 = (bf16[48,1280]{1,0:T(8,128)(2,1)S(1)}, bf16[48,1280]{1,0:T(8,128)(2,1)S(1)}, u32[]{:S(2)}, u32[]{:S(2)}) collective-permute-start(bf16[48,1280]{1,0:T(8,128)(2,1)S(1)} %get-tuple-element.34), channel_id=1, source_target_pairs={{0,97},{1,96},{32,1},{33,0},{64,33},{65,32},{96,65},{97,64},{2,99}... | collective-permute-start | bytes 368648 | tf_op jit(solution)/shard_map/ppermute | solution.py:111
  60.1 7.2 %collective-permute-start.11 = (bf16[48,1280]{1,0:T(8,128)(2,1)S(1)}, bf16[48,1280]{1,0:T(8,128)(2,1)S(1)}, u32[]{:S(2)}, u32[]{:S(2)}) collective-permute-start(bf16[48,1280]{1,0:T(8,128)(2,1)S(1)} %get-tuple-element.35), channel_id=1, source_target_pairs={{0,65},{1,64},{32,97},{33,96},{64,1},{65,0},{96,33},{97,32},{2,67}... | collective-permute-start | bytes 368648 | tf_op jit(solution)/shard_map/ppermute | solution.py:111
  60.1 9.7 %collective-permute-start.12 = (bf16[48,1280]{1,0:T(8,128)(2,1)S(1)}, bf16[48,1280]{1,0:T(8,128)(2,1)S(1)}, u32[]{:S(2)}, u32[]{:S(2)}) collective-permute-start(bf16[48,1280]{1,0:T(8,128)(2,1)S(1)} %get-tuple-element.36), channel_id=1, source_target_pairs={{0,33},{1,32},{32,65},{33,64},{64,97},{65,96},{96,1},{97,0},{2,35}... | collective-permute-start | bytes 368648 | tf_op jit(solution)/shard_map/ppermute | solution.py:111
  70.8 14.8 %collective-permute-start.13 = (bf16[384,1280]{1,0:T(8,128)(2,1)}, bf16[384,1280]{1,0:T(8,128)(2,1)}, u32[]{:S(2)}, u32[]{:S(2)}) collective-permute-start(bf16[384,1280]{1,0:T(8,128)(2,1)} %join.4), channel_id=1, source_target_pairs={{0,8},{1,3},{2,10},{3,5},{4,12},{5,7},{6,14},{7,1},{8,16},{9,11},{... | collective-permute-start | bytes 2949128 | tf_op jit(solution)/shard_map/ppermute | solution.py:33
  71.3 14.2 %collective-permute-start.14 = (bf16[384,1280]{1,0:T(8,128)(2,1)}, bf16[384,1280]{1,0:T(8,128)(2,1)S(1)}, u32[]{:S(2)}, u32[]{:S(2)}) collective-permute-start(bf16[384,1280]{1,0:T(8,128)(2,1)} %join.4), channel_id=1, source_target_pairs={{0,24},{1,7},{2,26},{3,1},{4,28},{5,3},{6,30},{7,5},{8,0},{9,15},{... | collective-permute-start | bytes 2949128 | tf_op jit(solution)/shard_map/ppermute | solution.py:33
  73.5 14.7 %collective-permute-start.2 = (bf16[8,48,624]{2,1,0:T(8,128)(2,1)S(1)}, bf16[8,48,624]{2,1,0:T(8,128)(2,1)S(1)}, u32[]{:S(2)}, u32[]{:S(2)}) collective-permute-start(bf16[8,48,624]{2,1,0:T(8,128)(2,1)S(1)} %slice.16), channel_id=1, source_target_pairs={{0,32},{32,64},{64,96},{96,0},{1,33},{33,65},{65,97},{97,1},{2,34}... | collective-permute-start | bytes 1437704 | tf_op jit(solution)/shard_map/ppermute | solution.py:19
  73.7 14.5 %collective-permute-start.3 = (bf16[8,48,624]{2,1,0:T(8,128)(2,1)S(1)}, bf16[8,48,624]{2,1,0:T(8,128)(2,1)S(1)}, u32[]{:S(2)}, u32[]{:S(2)}) collective-permute-start(bf16[8,48,624]{2,1,0:T(8,128)(2,1)S(1)} %slice.17), channel_id=1, source_target_pairs={{0,96},{32,0},{64,32},{96,64},{1,97},{33,1},{65,33},{97,65},{2,98}... | collective-permute-start | bytes 1437704 | tf_op jit(solution)/shard_map/ppermute | solution.py:19
  88.2 35.8 %collective-permute-start.18 = (bf16[768,1280]{1,0:T(8,128)(2,1)}, bf16[768,1280]{1,0:T(8,128)(2,1)}, u32[]{:S(2)}, u32[]{:S(2)}) collective-permute-start(bf16[768,1280]{1,0:T(8,128)(2,1)} %join.5), channel_id=1, source_target_pairs={{0,2},{1,9},{2,4},{3,11},{4,6},{5,13},{6,0},{7,15},{8,10},{9,17},{... | collective-permute-start | bytes 5898248 | tf_op jit(solution)/shard_map/ppermute | solution.py:33
  88.4 51.8 %collective-permute-start.5 = (bf16[48,48,624]{2,1,0:T(8,128)(2,1)S(1)}, bf16[48,48,624]{2,1,0:T(8,128)(2,1)}, u32[]{:S(2)}, u32[]{:S(2)}) collective-permute-start(bf16[48,48,624]{2,1,0:T(8,128)(2,1)S(1)} %join.3.refs_1_), channel_id=1, source_target_pairs={{0,1},{1,0},{2,3},{3,2},{4,5},{5,4},{6,7},{7,6},{8,9},{9,8},{10,11... | collective-permute-start | bytes 8626184 | tf_op jit(solution)/shard_map/ppermute | solution.py:23
  90.7 45.3 %collective-permute-start.19 = (bf16[768,1280]{1,0:T(8,128)(2,1)}, bf16[768,1280]{1,0:T(8,128)(2,1)}, u32[]{:S(2)}, u32[]{:S(2)}) collective-permute-start(bf16[768,1280]{1,0:T(8,128)(2,1)} %join.5), channel_id=1, source_target_pairs={{0,6},{1,25},{2,0},{3,27},{4,2},{5,29},{6,4},{7,31},{8,14},{9,1},{... | collective-permute-start | bytes 5898248 | tf_op jit(solution)/shard_map/ppermute | solution.py:33
  93.5 41.0 %collective-permute-start.16 = (bf16[384,1280]{1,0:T(8,128)(2,1)}, bf16[384,1280]{1,0:T(8,128)(2,1)}, u32[]{:S(2)}, u32[]{:S(2)}) collective-permute-start(bf16[384,1280]{1,0:T(8,128)(2,1)} %join.4), channel_id=1, source_target_pairs={{0,2},{1,9},{2,4},{3,11},{4,6},{5,13},{6,0},{7,15},{8,10},{9,17},{... | collective-permute-start | bytes 2949128 | tf_op jit(solution)/shard_map/ppermute | solution.py:33
  93.5 41.0 %collective-permute-start.15 = (bf16[384,1280]{1,0:T(8,128)(2,1)}, bf16[384,1280]{1,0:T(8,128)(2,1)}, u32[]{:S(2)}, u32[]{:S(2)}) collective-permute-start(bf16[384,1280]{1,0:T(8,128)(2,1)} %collective-permute-done.13.refs_0_), channel_id=1, source_target_pairs={{0,8},{1,3},{2,10},{3,5},{4,12},{5,7},{6,14},{7,1},{8,16},{9,11},{... | collective-permute-start | bytes 2949128 | tf_op jit(solution)/shard_map/ppermute | solution.py:33
  124.0 13.6 %collective-permute-start.4 = (bf16[16,48,624]{2,1,0:T(8,128)(2,1)}, bf16[16,48,624]{2,1,0:T(8,128)(2,1)}, u32[]{:S(2)}, u32[]{:S(2)}) collective-permute-start(bf16[16,48,624]{2,1,0:T(8,128)(2,1)} %all_to_all.5.refs_0_), channel_id=1, source_target_pairs={{0,1},{1,0},{2,3},{3,2},{4,5},{5,4},{6,7},{7,6},{8,9},{9,8},{10,11... | collective-permute-start | bytes 2875400 | tf_op jit(solution)/shard_map/ppermute | solution.py:23
  134.5 22.2 %collective-permute-start.17 = (bf16[384,1280]{1,0:T(8,128)(2,1)}, bf16[384,1280]{1,0:T(8,128)(2,1)S(1)}, u32[]{:S(2)}, u32[]{:S(2)}) collective-permute-start(bf16[384,1280]{1,0:T(8,128)(2,1)} %join.4), channel_id=1, source_target_pairs={{0,6},{1,25},{2,0},{3,27},{4,2},{5,29},{6,4},{7,31},{8,14},{9,1},{... | collective-permute-start | bytes 2949128 | tf_op jit(solution)/shard_map/ppermute | solution.py:33
  134.5 30.4 %collective-permute-start.20 = (bf16[384,1280]{1,0:T(8,128)(2,1)}, bf16[384,1280]{1,0:T(8,128)(2,1)S(1)}, u32[]{:S(2)}, u32[]{:S(2)}) collective-permute-start(bf16[384,1280]{1,0:T(8,128)(2,1)} %collective-permute-done.16), channel_id=1, source_target_pairs={{0,2},{1,9},{2,4},{3,11},{4,6},{5,13},{6,0},{7,15},{8,10},{9,17},{... | collective-permute-start | bytes 2949128 | tf_op jit(solution)/shard_map/ppermute | solution.py:33
  136.0 30.0 %collective-permute-start.21 = (bf16[384,1280]{1,0:T(8,128)(2,1)}, bf16[384,1280]{1,0:T(8,128)(2,1)S(1)}, u32[]{:S(2)}, u32[]{:S(2)}) collective-permute-start(bf16[384,1280]{1,0:T(8,128)(2,1)} %collective-permute-done.15), channel_id=1, source_target_pairs={{0,2},{1,9},{2,4},{3,11},{4,6},{5,13},{6,0},{7,15},{8,10},{9,17},{... | collective-permute-start | bytes 2949128 | tf_op jit(solution)/shard_map/ppermute | solution.py:33
  137.6 21.9 %collective-permute-start.22 = (bf16[384,1280]{1,0:T(8,128)(2,1)}, bf16[384,1280]{1,0:T(8,128)(2,1)S(1)}, u32[]{:S(2)}, u32[]{:S(2)}) collective-permute-start(bf16[384,1280]{1,0:T(8,128)(2,1)} %collective-permute-done.15), channel_id=1, source_target_pairs={{0,6},{1,25},{2,0},{3,27},{4,2},{5,29},{6,4},{7,31},{8,14},{9,1},{... | collective-permute-start | bytes 2949128 | tf_op jit(solution)/shard_map/ppermute | solution.py:33
  140.2 28.3 %collective-permute-start.23 = (bf16[192,1280]{1,0:T(8,128)(2,1)S(1)}, bf16[192,1280]{1,0:T(8,128)(2,1)S(1)}, u32[]{:S(2)}, u32[]{:S(2)}) collective-permute-start(bf16[192,1280]{1,0:T(8,128)(2,1)S(1)} %slice.18), channel_id=1, source_target_pairs={{0,2},{1,9},{2,4},{3,11},{4,6},{5,13},{6,0},{7,15},{8,10},{9,17},{... | collective-permute-start | bytes 1474568 | tf_op jit(solution)/shard_map/ppermute | solution.py:33
  156.7 19.1 %collective-permute-start.24 = (bf16[576,1280]{1,0:T(8,128)(2,1)S(1)}, bf16[576,1280]{1,0:T(8,128)(2,1)S(1)}, u32[]{:S(2)}, u32[]{:S(2)}) collective-permute-start(bf16[576,1280]{1,0:T(8,128)(2,1)S(1)} %slice.19), channel_id=1, source_target_pairs={{0,6},{1,25},{2,0},{3,27},{4,2},{5,29},{6,4},{7,31},{8,14},{9,1},{... | collective-permute-start | bytes 4423688 | tf_op jit(solution)/shard_map/ppermute | solution.py:33
  159.4 26.8 %collective-permute-start.25 = (bf16[384,1280]{1,0:T(8,128)(2,1)S(1)}, bf16[384,1280]{1,0:T(8,128)(2,1)S(1)}, u32[]{:S(2)}, u32[]{:S(2)}) collective-permute-start(bf16[384,1280]{1,0:T(8,128)(2,1)S(1)} %collective-permute-done.22), channel_id=1, source_target_pairs={{0,6},{1,25},{2,0},{3,27},{4,2},{5,29},{6,4},{7,31},{8,14},{9,1},{... | collective-permute-start | bytes 2949128 | tf_op jit(solution)/shard_map/ppermute | solution.py:33
  187.5 7.6 %collective-permute-start.26 = (f32[312,1280]{1,0:T(8,128)S(1)}, f32[312,1280]{1,0:T(8,128)S(1)}, u32[]{:S(2)}, u32[]{:S(2)}) collective-permute-start(f32[312,1280]{1,0:T(8,128)S(1)} %dynamic-slice_bitcast_fusion), channel_id=1, source_target_pairs={{0,1},{1,0},{2,3},{3,2},{4,5},{5,4},{6,7},{7,6},{8,9},{9,8},{10,11... | collective-permute-start | bytes 4792328 | tf_op jit(solution)/shard_map/ppermute | solution.py:23
where the time goes:
time: 198 us; the launch traced here: 197 us
  waiting for transfers between devices  93.5 us (47%)
  starting transfers between devices  39.2 us (20%)
  blocking collectives  23.6 us (12%)
  matrix products  22.9 us (12%)
  Pallas kernels  9.84 us (5%)
  local copies, waits for them, and re-layouts  4.58 us (2%)
  other arithmetic  3.19 us (2%)
    ppermute x13, waiting for transfers between devices, along_plane(): return lax.ppermute(block, ('x', 'z', 'core'), route)  61.7 us
    ppermute x7, waiting for transfers between devices, exchanged(): block = lax.ppermute(block, ('y', 'core'), route)  28.8 us
    all_to_all x1, blocking collectives, body(): rows = lax.all_to_all(rows, ('x', 'z'), 0, 0, tiled=True)  23.6 us
    dot_general x13, matrix products, body(): lax.dot_general(weight, block, (((0,), (0,)), ((), ())), preferred_elemen...  22.9 us
    ppermute x13, starting transfers between devices, along_plane(): return lax.ppermute(block, ('x', 'z', 'core'), route)  12.9 us
    ppermute x7, starting transfers between devices, exchanged(): block = lax.ppermute(block, ('y', 'core'), route)  11.7 us
    ppermute x3, starting transfers between devices, swap_cores(): return lax.ppermute(block, 'core', [(0, 1), (1, 0)])  9.07 us
    ppermute x4, starting transfers between devices, along_y(): lax.ppermute(block, 'y', [(i, (i + step) % SIDE) for i in range(SIDE)])  5.53 us
  transfers between devices with their start and end apart: 27, of which 10 were waited for; matrix products, arithmetic and copies ran while one was open for 14% of the time, Pallas kernels for 3%

commit v1 on v0

--- a/solution.py
+++ b/solution.py
@@ -48,7 +48,7 @@
         out_shape=joined,
         in_specs=[VMEM] * len(blocks),
         out_specs=VMEM,
-        compiler_params=pltpu.CompilerParams(vmem_limit_bytes=4 * size),
+        compiler_params=pltpu.CompilerParams(vmem_limit_bytes=2 * size + (1 << 18)),
         cost_estimate=pl.CostEstimate(flops=0, bytes_accessed=2 * size, transcendentals=0),
         name="join",
     )(*blocks)
@@ -161,38 +161,58 @@
         out_shape=tuple(jax.ShapeDtypeStruct((len(blocks) * depth, chip_rows), rows.dtype) for blocks in layout),
         in_specs=[VMEM] * 4,
         out_specs=(VMEM,) * len(layout),
-        compiler_params=pltpu.CompilerParams(vmem_limit_bytes=20 << 20),
+        compiler_params=pltpu.CompilerParams(vmem_limit_bytes=16 << 20),
         name="arrange",
     )(rows, rest, other_rows, other_rest)
 
 
-def assemble_kernel(tile_ref, got_ref, out_ref):
+def halve_kernel(tile_ref, kept_ref, sent_ref):
+    rows = kept_ref.shape[0]
+    for core in range(CORES):
+
+        @pl.when(lax.axis_index("core") == core)
+        def _():
+            kept_ref[...] = tile_ref[core * rows : (core + 1) * rows, :]
+            sent_ref[...] = tile_ref[(1 - core) * rows : (2 - core) * rows, :]
+
+
+def halve(tile):
+    half = jax.ShapeDtypeStruct((tile.shape[0] // CORES, tile.shape[1]), tile.dtype)
+    return pl.pallas_call(
+        halve_kernel,
+        out_shape=(half, half),
+        in_specs=[VMEM],
+        out_specs=(VMEM, VMEM),
+        compiler_params=pltpu.CompilerParams(vmem_limit_bytes=8 << 20),
+        name="halve",
+    )(tile)
+
+
+def assemble_kernel(kept_ref, got_ref, out_ref):
     rest = out_ref.shape[1] - WIDE
     for core in range(CORES):
 
         @pl.when(lax.axis_index("core") == core)
         def _():
-            first, last = (tile_ref.at[core], got_ref) if core == 0 else (got_ref, tile_ref.at[core])
+            first, last = (kept_ref, got_ref) if core == 0 else (got_ref, kept_ref)
             out_ref[:, :WIDE] = first[...]
             out_ref[:, WIDE:] = last[:, :rest]
 
 
-def assemble(tile, got, columns):
+def assemble(kept, got, columns):
     return pl.pallas_call(
         assemble_kernel,
         out_shape=jax.ShapeDtypeStruct((got.shape[0], columns), got.dtype),
         in_specs=[VMEM, VMEM],
         out_specs=VMEM,
-        compiler_params=pltpu.CompilerParams(vmem_limit_bytes=20 << 20),
+        compiler_params=pltpu.CompilerParams(vmem_limit_bytes=8 << 20),
         name="assemble",
-    )(tile, got)
+    )(kept, got)
 
 
 def body(b_tensor, aux_counts):
     basis = b_tensor.shape[0]
-    core = lax.axis_index("core")
     windows, rows = pack(aux_counts, b_tensor.transpose(1, 2, 0))
-    chip_rows = rows.shape[2]
 
     columns = exchanged(windows)
     rows = lax.all_to_all(rows, ("x", "z"), 0, 0, tiled=True)
@@ -216,9 +236,8 @@
         product = lax.dot_general(weight, block, (((0,), (0,)), ((), ())), preferred_element_type=jnp.float32)
         tile = lax.optimization_barrier(product if tile is None else tile + product)
 
-    tile = tile.reshape(CORES, chip_rows // CORES, WIDE)
-    got = swap_cores(lax.dynamic_index_in_dim(tile, 1 - core, 0, keepdims=False))
-    return assemble(tile, got, basis // SIDE)
+    kept, sent = halve(tile)
+    return assemble(kept, swap_cores(sent), basis // SIDE)
 
 
 def solution(mesh):

time: 198 us -> 190 us (0.960)
  waiting for transfers between devices: 93.5 us -> 106 us
  matrix products: 22.9 us -> 14.6 us
  Pallas kernels: 9.84 us -> 4.25 us
  starting transfers between devices: 39.2 us -> 36.4 us
  local copies, waits for them, and re-layouts: 4.58 us -> 2.06 us
    ppermute x13, waiting for transfers between devices: 61.7 us -> 73 us  [along_plane(): return lax.ppermute(block, ('x', 'z', 'core'), route)]
    dot_general x13, matrix products: 22.9 us -> 14.6 us  [body(): lax.dot_general(weight, block, (((0,), (0,)), ((), ())), preferred_elemen...]
    pallas_call x3, Pallas kernels: 3.85 us -> 0.42 us  [join(): pl.pallas_call(kernel, out_shape=joined, in_specs=[VMEM] * len(blocks), o...]
    pallas_call x1, Pallas kernels: 3 us -> 0.61 us  [arrange(): pl.pallas_call(lambda *refs: arrange_kernel(layout, *refs), out_shape=tup...]
  transfers between devices with their start and end apart: 27 -> 27, of which waited for: 10 -> 13; matrix products, arithmetic and copies ran while one was open for 14% -> 9% of each run, Pallas kernels for 3% -> 1%
where the time goes in v1:
time: 190 us
  waiting for transfers between devices  106 us (56%)
  starting transfers between devices  36.4 us (19%)
  blocking collectives  23.5 us (12%)
  matrix products  14.6 us (8%)
  Pallas kernels  4.25 us (2%)
  other arithmetic  3.13 us (2%)
  local copies, waits for them, and re-layouts  2.06 us (1%)
    ppermute x13, waiting for transfers between devices, along_plane(): return lax.ppermute(block, ('x', 'z', 'core'), route)  73 us
    ppermute x7, waiting for transfers between devices, exchanged(): block = lax.ppermute(block, ('y', 'core'), route)  28.6 us
    all_to_all x1, blocking collectives, body(): rows = lax.all_to_all(rows, ('x', 'z'), 0, 0, tiled=True)  23.5 us
    dot_general x13, matrix products, body(): lax.dot_general(weight, block, (((0,), (0,)), ((), ())), preferred_elemen...  14.6 us
    ppermute x13, starting transfers between devices, along_plane(): return lax.ppermute(block, ('x', 'z', 'core'), route)  11.7 us
    ppermute x7, starting transfers between devices, exchanged(): block = lax.ppermute(block, ('y', 'core'), route)  11.7 us
    ppermute x3, starting transfers between devices, swap_cores(): return lax.ppermute(block, 'core', [(0, 1), (1, 0)])  7.43 us
    ppermute x4, starting transfers between devices, along_y(): lax.ppermute(block, 'y', [(i, (i + step) % SIDE) for i in range(SIDE)])  5.53 us
  transfers between devices with their start and end apart: 27, of which 13 were waited for; matrix products, arithmetic and copies ran while one was open for 9% of the time, Pallas kernels for 1%

profile of v1, /device:TPU:1, one launch (start us, length us, event | category | flops | bytes accessed | tf_op | source)
XLA Modules:
  0.0 189.9 jit_solution(9674509555387074243)
XLA Ops:
  3.0 23.5 %all_to_all.5.refs_0_ = bf16[16,48,624]{2,1,0:T(8,128)(2,1)S(1)} all-to-all(bf16[16,48,624]{2,1,0:T(8,128)(2,1)S(1)} %get-tuple-element.29), channel_id=1, replica_groups=mesh['y'=4,'x'=4,'z'=4,'core'=2] {'x','z'}, dimensions={0} | all-to-all | bytes 1916928 | tf_op jit(solution)/shard_map/all_to_all | solution.py:218
  26.5 1.3 collective-permute-start.1
  27.8 1.4 collective-permute-start
  29.2 1.5 collective-permute-start.6
  31.7 19.9 %collective-permute-done.6.refs_1_ = bf16[48,1280]{1,0:T(8,128)(2,1)S(1)} collective-permute-done((bf16[48,1280]{1,0:T(8,128)(2,1)S(1)}, bf16[48,1280]{1,0:T(8,128)(2,1)S(1)}, u32[]{:S(2)}, u32[]{:S(2)}) %collective-permute-start.6) | collective-permute-done | bytes 122912 | tf_op jit(solution)/shard_map/ppermute | solution.py:111
  51.6 4.3 %collective-permute-start.9 = (bf16[48,1280]{1,0:T(8,128)(2,1)S(1)}, bf16[48,1280]{1,0:T(8,128)(2,1)S(1)}, u32[]{:S(2)}, u32[]{:S(2)}) collective-permute-start(bf16[48,1280]{1,0:T(8,128)(2,1)S(1)} %get-tuple-element.35), channel_id=1, source_target_pairs={{0,1},{1,0},{32,33},{33,32},{64,65},{65,64},{96,97},{97,96},{2,3},... | collective-permute-start | bytes 368648 | tf_op jit(solution)/shard_map/ppermute | solution.py:111
  55.9 3.9 %collective-permute-start.10 = (bf16[48,1280]{1,0:T(8,128)(2,1)S(1)}, bf16[48,1280]{1,0:T(8,128)(2,1)S(1)}, u32[]{:S(2)}, u32[]{:S(2)}) collective-permute-start(bf16[48,1280]{1,0:T(8,128)(2,1)S(1)} %get-tuple-element.36), channel_id=1, source_target_pairs={{0,97},{1,96},{32,1},{33,0},{64,33},{65,32},{96,65},{97,64},{2,99}... | collective-permute-start | bytes 368648 | tf_op jit(solution)/shard_map/ppermute | solution.py:111
  60.8 4.0 %collective-permute-done.10.refs_5_ = bf16[48,1280]{1,0:T(8,128)(2,1)S(1)} collective-permute-done((bf16[48,1280]{1,0:T(8,128)(2,1)S(1)}, bf16[48,1280]{1,0:T(8,128)(2,1)S(1)}, u32[]{:S(2)}, u32[]{:S(2)}) %collective-permute-start.10) | collective-permute-done | bytes 122912 | tf_op jit(solution)/shard_map/ppermute | solution.py:111
  64.8 2.1 %collective-permute-done.11.refs_6_ = bf16[48,1280]{1,0:T(8,128)(2,1)S(1)} collective-permute-done((bf16[48,1280]{1,0:T(8,128)(2,1)S(1)}, bf16[48,1280]{1,0:T(8,128)(2,1)S(1)}, u32[]{:S(2)}, u32[]{:S(2)}) %collective-permute-start.11) | collective-permute-done | bytes 122912 | tf_op jit(solution)/shard_map/ppermute | solution.py:111
  66.9 2.5 %collective-permute-done.12.refs_7_ = bf16[48,1280]{1,0:T(8,128)(2,1)S(1)} collective-permute-done((bf16[48,1280]{1,0:T(8,128)(2,1)S(1)}, bf16[48,1280]{1,0:T(8,128)(2,1)S(1)}, u32[]{:S(2)}, u32[]{:S(2)}) %collective-permute-start.12) | collective-permute-done | bytes 122912 | tf_op jit(solution)/shard_map/ppermute | solution.py:111
  70.1 2.1 %collective-permute-start.14 = (bf16[384,1280]{1,0:T(8,128)(2,1)S(1)}, bf16[384,1280]{1,0:T(8,128)(2,1)S(1)}, u32[]{:S(2)}, u32[]{:S(2)}) collective-permute-start(bf16[384,1280]{1,0:T(8,128)(2,1)S(1)} %join.4), channel_id=1, source_target_pairs={{0,24},{1,7},{2,26},{3,1},{4,28},{5,3},{6,30},{7,5},{8,0},{9,15},{... | collective-permute-start | bytes 2949128 | tf_op jit(solution)/shard_map/ppermute | solution.py:33
  72.5 2.7 %collective-permute-start.3 = (bf16[8,48,624]{2,1,0:T(8,128)(2,1)S(1)}, bf16[8,48,624]{2,1,0:T(8,128)(2,1)S(1)}, u32[]{:S(2)}, u32[]{:S(2)}) collective-permute-start(bf16[8,48,624]{2,1,0:T(8,128)(2,1)S(1)} %slice.17), channel_id=1, source_target_pairs={{0,96},{32,0},{64,32},{96,64},{1,97},{33,1},{65,33},{97,65},{2,98}... | collective-permute-start | bytes 1437704 | tf_op jit(solution)/shard_map/ppermute | solution.py:19
  75.2 8.9 %collective-permute-done.13.refs_0_ = bf16[384,1280]{1,0:T(8,128)(2,1)S(1)} collective-permute-done((bf16[384,1280]{1,0:T(8,128)(2,1)S(1)}, bf16[384,1280]{1,0:T(8,128)(2,1)S(1)}, u32[]{:S(2)}, u32[]{:S(2)}) %collective-permute-start.13) | collective-permute-done | bytes 983072 | tf_op jit(solution)/shard_map/ppermute | solution.py:33
  85.5 2.0 %collective-permute-start.5 = (bf16[48,48,624]{2,1,0:T(8,128)(2,1)S(1)}, bf16[48,48,624]{2,1,0:T(8,128)(2,1)S(1)}, u32[]{:S(2)}, u32[]{:S(2)}) collective-permute-start(bf16[48,48,624]{2,1,0:T(8,128)(2,1)S(1)} %join.3.refs_1_), channel_id=1, source_target_pairs={{0,1},{1,0},{2,3},{3,2},{4,5},{5,4},{6,7},{7,6},{8,9},{9,8},{10,11... | collective-permute-start | bytes 8626184 | tf_op jit(solution)/shard_map/ppermute | solution.py:23
  87.5 2.2 %collective-permute-start.19 = (bf16[768,1280]{1,0:T(8,128)(2,1)S(1)}, bf16[768,1280]{1,0:T(8,128)(2,1)S(1)}, u32[]{:S(2)}, u32[]{:S(2)}) collective-permute-start(bf16[768,1280]{1,0:T(8,128)(2,1)S(1)} %join.5), channel_id=1, source_target_pairs={{0,6},{1,25},{2,0},{3,27},{4,2},{5,29},{6,4},{7,31},{8,14},{9,1},{... | collective-permute-start | bytes 5898248 | tf_op jit(solution)/shard_map/ppermute | solution.py:33
  89.8 30.0 %collective-permute-done.18 = bf16[768,1280]{1,0:T(8,128)(2,1)S(1)} collective-permute-done((bf16[768,1280]{1,0:T(8,128)(2,1)S(1)}, bf16[768,1280]{1,0:T(8,128)(2,1)S(1)}, u32[]{:S(2)}, u32[]{:S(2)}) %collective-permute-start.18) | collective-permute-done | bytes 1966112 | tf_op jit(solution)/shard_map/ppermute | solution.py:33
  119.8 2.2 %collective-permute-start.4 = (bf16[16,48,624]{2,1,0:T(8,128)(2,1)S(1)}, bf16[16,48,624]{2,1,0:T(8,128)(2,1)S(1)}, u32[]{:S(2)}, u32[]{:S(2)}) collective-permute-start(bf16[16,48,624]{2,1,0:T(8,128)(2,1)S(1)} %all_to_all.5.refs_0_), channel_id=1, source_target_pairs={{0,1},{1,0},{2,3},{3,2},{4,5},{5,4},{6,7},{7,6},{8,9},{9,8},{10,11... | collective-permute-start | bytes 2875400 | tf_op jit(solution)/shard_map/ppermute | solution.py:23
  122.0 8.3 %collective-permute-done.16 = bf16[384,1280]{1,0:T(8,128)(2,1)S(1)} collective-permute-done((bf16[384,1280]{1,0:T(8,128)(2,1)S(1)}, bf16[384,1280]{1,0:T(8,128)(2,1)S(1)}, u32[]{:S(2)}, u32[]{:S(2)}) %collective-permute-start.16) | collective-permute-done | bytes 983072 | tf_op jit(solution)/shard_map/ppermute | solution.py:33
  130.3 1.5 collective-permute-start.20
  132.0 2.7 %collective-permute-start.22 = (bf16[384,1280]{1,0:T(8,128)(2,1)S(1)}, bf16[384,1280]{1,0:T(8,128)(2,1)S(1)}, u32[]{:S(2)}, u32[]{:S(2)}) collective-permute-start(bf16[384,1280]{1,0:T(8,128)(2,1)S(1)} %collective-permute-done.15), channel_id=1, source_target_pairs={{0,6},{1,25},{2,0},{3,27},{4,2},{5,29},{6,4},{7,31},{8,14},{9,1},{... | collective-permute-start | bytes 2949128 | tf_op jit(solution)/shard_map/ppermute | solution.py:33
  136.3 1.4 fusion.1
  140.6 1.4 fusion.4
  142.0 1.5 collective-permute-done.17
  143.5 1.2 collective-permute-start.24
  144.8 9.3 %collective-permute-done.22 = bf16[384,1280]{1,0:T(8,128)(2,1)S(1)} collective-permute-done((bf16[384,1280]{1,0:T(8,128)(2,1)S(1)}, bf16[384,1280]{1,0:T(8,128)(2,1)S(1)}, u32[]{:S(2)}, u32[]{:S(2)}) %collective-permute-start.22) | collective-permute-done | bytes 983072 | tf_op jit(solution)/shard_map/ppermute | solution.py:33
  157.1 1.4 fusion.5
  163.5 6.4 %collective-permute-done.24 = bf16[576,1280]{1,0:T(8,128)(2,1)S(1)} collective-permute-done((bf16[576,1280]{1,0:T(8,128)(2,1)S(1)}, bf16[576,1280]{1,0:T(8,128)(2,1)S(1)}, u32[]{:S(2)}, u32[]{:S(2)}) %collective-permute-start.24) | collective-permute-done | bytes 1474592 | tf_op jit(solution)/shard_map/ppermute | solution.py:33
  169.9 1.4 fusion.8
  171.7 8.7 %collective-permute-done.25 = bf16[384,1280]{1,0:T(8,128)(2,1)S(1)} collective-permute-done((bf16[384,1280]{1,0:T(8,128)(2,1)S(1)}, bf16[384,1280]{1,0:T(8,128)(2,1)S(1)}, u32[]{:S(2)}, u32[]{:S(2)}) %collective-permute-start.25) | collective-permute-done | bytes 983072 | tf_op jit(solution)/shard_map/ppermute | solution.py:33
  181.7 3.2 %collective-permute-start.26 = (f32[312,1280]{1,0:T(8,128)S(1)}, f32[312,1280]{1,0:T(8,128)S(1)}, u32[]{:S(2)}, u32[]{:S(2)}) collective-permute-start(f32[312,1280]{1,0:T(8,128)S(1)} %get-tuple-element.52), channel_id=1, source_target_pairs={{0,1},{1,0},{2,3},{3,2},{4,5},{5,4},{6,7},{7,6},{8,9},{9,8},{10,11... | collective-permute-start | bytes 4792328 | tf_op jit(solution)/shard_map/ppermute | solution.py:23
  184.9 3.1 %collective-permute-done.26.got_ref = f32[312,1280]{1,0:T(8,128)S(1)} collective-permute-done((f32[312,1280]{1,0:T(8,128)S(1)}, f32[312,1280]{1,0:T(8,128)S(1)}, u32[]{:S(2)}, u32[]{:S(2)}) %collective-permute-start.26) | collective-permute-done | bytes 1597472 | tf_op jit(solution)/shard_map/ppermute | solution.py:23
  188.0 1.9 assemble.1
  (59 shorter events, 21.7 us)
Async XLA Ops:
  0.0 1.2 copy-start
  1.2 0.7 copy-start.1
  26.5 45.8 %collective-permute-start.1 = (bf16[16,48,624]{2,1,0:T(8,128)(2,1)S(1)}, bf16[16,48,624]{2,1,0:T(8,128)(2,1)S(1)}, u32[]{:S(2)}, u32[]{:S(2)}) collective-permute-start(bf16[16,48,624]{2,1,0:T(8,128)(2,1)S(1)} %all_to_all.5.refs_0_), channel_id=1, source_target_pairs={{0,32},{32,64},{64,96},{96,0},{1,33},{33,65},{65,97},{97,1},{2,34}... | collective-permute-start | bytes 2875400 | tf_op jit(solution)/shard_map/ppermute | solution.py:19
  27.8 44.6 %collective-permute-start = (bf16[16,48,624]{2,1,0:T(8,128)(2,1)S(1)}, bf16[16,48,624]{2,1,0:T(8,128)(2,1)S(1)}, u32[]{:S(2)}, u32[]{:S(2)}) collective-permute-start(bf16[16,48,624]{2,1,0:T(8,128)(2,1)S(1)} %all_to_all.5.refs_0_), channel_id=1, source_target_pairs={{0,96},{32,0},{64,32},{96,64},{1,97},{33,1},{65,33},{97,65},{2,98}... | collective-permute-start | bytes 2875400 | tf_op jit(solution)/shard_map/ppermute | solution.py:19
  29.2 22.4 %collective-permute-start.6 = (bf16[48,1280]{1,0:T(8,128)(2,1)S(1)}, bf16[48,1280]{1,0:T(8,128)(2,1)S(1)}, u32[]{:S(2)}, u32[]{:S(2)}) collective-permute-start(bf16[48,1280]{1,0:T(8,128)(2,1)S(1)} %get-tuple-element.32), channel_id=1, source_target_pairs={{0,96},{1,97},{32,0},{33,1},{64,32},{65,33},{96,64},{97,65},{2,98}... | collective-permute-start | bytes 368648 | tf_op jit(solution)/shard_map/ppermute | solution.py:111
  30.7 25.2 %collective-permute-start.7 = (bf16[48,1280]{1,0:T(8,128)(2,1)S(1)}, bf16[48,1280]{1,0:T(8,128)(2,1)S(1)}, u32[]{:S(2)}, u32[]{:S(2)}) collective-permute-start(bf16[48,1280]{1,0:T(8,128)(2,1)S(1)} %get-tuple-element.33), channel_id=1, source_target_pairs={{0,64},{1,65},{32,96},{33,97},{64,0},{65,1},{96,32},{97,33},{2,66}... | collective-permute-start | bytes 368648 | tf_op jit(solution)/shard_map/ppermute | solution.py:111
  31.0 28.7 %collective-permute-start.8 = (bf16[48,1280]{1,0:T(8,128)(2,1)S(1)}, bf16[48,1280]{1,0:T(8,128)(2,1)S(1)}, u32[]{:S(2)}, u32[]{:S(2)}) collective-permute-start(bf16[48,1280]{1,0:T(8,128)(2,1)S(1)} %get-tuple-element.34), channel_id=1, source_target_pairs={{0,32},{1,33},{32,64},{33,65},{64,96},{65,97},{96,0},{97,1},{2,34}... | collective-permute-start | bytes 368648 | tf_op jit(solution)/shard_map/ppermute | solution.py:111
  51.6 8.1 %collective-permute-start.9 = (bf16[48,1280]{1,0:T(8,128)(2,1)S(1)}, bf16[48,1280]{1,0:T(8,128)(2,1)S(1)}, u32[]{:S(2)}, u32[]{:S(2)}) collective-permute-start(bf16[48,1280]{1,0:T(8,128)(2,1)S(1)} %get-tuple-element.35), channel_id=1, source_target_pairs={{0,1},{1,0},{32,33},{33,32},{64,65},{65,64},{96,97},{97,96},{2,3},... | collective-permute-start | bytes 368648 | tf_op jit(solution)/shard_map/ppermute | solution.py:111
  55.9 8.9 %collective-permute-start.10 = (bf16[48,1280]{1,0:T(8,128)(2,1)S(1)}, bf16[48,1280]{1,0:T(8,128)(2,1)S(1)}, u32[]{:S(2)}, u32[]{:S(2)}) collective-permute-start(bf16[48,1280]{1,0:T(8,128)(2,1)S(1)} %get-tuple-element.36), channel_id=1, source_target_pairs={{0,97},{1,96},{32,1},{33,0},{64,33},{65,32},{96,65},{97,64},{2,99}... | collective-permute-start | bytes 368648 | tf_op jit(solution)/shard_map/ppermute | solution.py:111
  59.7 7.2 %collective-permute-start.11 = (bf16[48,1280]{1,0:T(8,128)(2,1)S(1)}, bf16[48,1280]{1,0:T(8,128)(2,1)S(1)}, u32[]{:S(2)}, u32[]{:S(2)}) collective-permute-start(bf16[48,1280]{1,0:T(8,128)(2,1)S(1)} %get-tuple-element.37), channel_id=1, source_target_pairs={{0,65},{1,64},{32,97},{33,96},{64,1},{65,0},{96,33},{97,32},{2,67}... | collective-permute-start | bytes 368648 | tf_op jit(solution)/shard_map/ppermute | solution.py:111
  59.8 9.7 %collective-permute-start.12 = (bf16[48,1280]{1,0:T(8,128)(2,1)S(1)}, bf16[48,1280]{1,0:T(8,128)(2,1)S(1)}, u32[]{:S(2)}, u32[]{:S(2)}) collective-permute-start(bf16[48,1280]{1,0:T(8,128)(2,1)S(1)} %get-tuple-element.38), channel_id=1, source_target_pairs={{0,33},{1,32},{32,65},{33,64},{64,97},{65,96},{96,1},{97,0},{2,35}... | collective-permute-start | bytes 368648 | tf_op jit(solution)/shard_map/ppermute | solution.py:111
  69.5 14.5 %collective-permute-start.13 = (bf16[384,1280]{1,0:T(8,128)(2,1)S(1)}, bf16[384,1280]{1,0:T(8,128)(2,1)S(1)}, u32[]{:S(2)}, u32[]{:S(2)}) collective-permute-start(bf16[384,1280]{1,0:T(8,128)(2,1)S(1)} %join.4), channel_id=1, source_target_pairs={{0,8},{1,3},{2,10},{3,5},{4,12},{5,7},{6,14},{7,1},{8,16},{9,11},{... | collective-permute-start | bytes 2949128 | tf_op jit(solution)/shard_map/ppermute | solution.py:33
  70.1 13.9 %collective-permute-start.14 = (bf16[384,1280]{1,0:T(8,128)(2,1)S(1)}, bf16[384,1280]{1,0:T(8,128)(2,1)S(1)}, u32[]{:S(2)}, u32[]{:S(2)}) collective-permute-start(bf16[384,1280]{1,0:T(8,128)(2,1)S(1)} %join.4), channel_id=1, source_target_pairs={{0,24},{1,7},{2,26},{3,1},{4,28},{5,3},{6,30},{7,5},{8,0},{9,15},{... | collective-permute-start | bytes 2949128 | tf_op jit(solution)/shard_map/ppermute | solution.py:33
  72.3 13.0 %collective-permute-start.2 = (bf16[8,48,624]{2,1,0:T(8,128)(2,1)S(1)}, bf16[8,48,624]{2,1,0:T(8,128)(2,1)S(1)}, u32[]{:S(2)}, u32[]{:S(2)}) collective-permute-start(bf16[8,48,624]{2,1,0:T(8,128)(2,1)S(1)} %slice.16), channel_id=1, source_target_pairs={{0,32},{32,64},{64,96},{96,0},{1,33},{33,65},{65,97},{97,1},{2,34}... | collective-permute-start | bytes 1437704 | tf_op jit(solution)/shard_map/ppermute | solution.py:19
  72.5 12.8 %collective-permute-start.3 = (bf16[8,48,624]{2,1,0:T(8,128)(2,1)S(1)}, bf16[8,48,624]{2,1,0:T(8,128)(2,1)S(1)}, u32[]{:S(2)}, u32[]{:S(2)}) collective-permute-start(bf16[8,48,624]{2,1,0:T(8,128)(2,1)S(1)} %slice.17), channel_id=1, source_target_pairs={{0,96},{32,0},{64,32},{96,64},{1,97},{33,1},{65,33},{97,65},{2,98}... | collective-permute-start | bytes 1437704 | tf_op jit(solution)/shard_map/ppermute | solution.py:19
  84.2 35.6 %collective-permute-start.18 = (bf16[768,1280]{1,0:T(8,128)(2,1)S(1)}, bf16[768,1280]{1,0:T(8,128)(2,1)S(1)}, u32[]{:S(2)}, u32[]{:S(2)}) collective-permute-start(bf16[768,1280]{1,0:T(8,128)(2,1)S(1)} %join.5), channel_id=1, source_target_pairs={{0,2},{1,9},{2,4},{3,11},{4,6},{5,13},{6,0},{7,15},{8,10},{9,17},{... | collective-permute-start | bytes 5898248 | tf_op jit(solution)/shard_map/ppermute | solution.py:33
  85.5 49.1 %collective-permute-start.5 = (bf16[48,48,624]{2,1,0:T(8,128)(2,1)S(1)}, bf16[48,48,624]{2,1,0:T(8,128)(2,1)S(1)}, u32[]{:S(2)}, u32[]{:S(2)}) collective-permute-start(bf16[48,48,624]{2,1,0:T(8,128)(2,1)S(1)} %join.3.refs_1_), channel_id=1, source_target_pairs={{0,1},{1,0},{2,3},{3,2},{4,5},{5,4},{6,7},{7,6},{8,9},{9,8},{10,11... | collective-permute-start | bytes 8626184 | tf_op jit(solution)/shard_map/ppermute | solution.py:23
  87.5 44.2 %collective-permute-start.19 = (bf16[768,1280]{1,0:T(8,128)(2,1)S(1)}, bf16[768,1280]{1,0:T(8,128)(2,1)S(1)}, u32[]{:S(2)}, u32[]{:S(2)}) collective-permute-start(bf16[768,1280]{1,0:T(8,128)(2,1)S(1)} %join.5), channel_id=1, source_target_pairs={{0,6},{1,25},{2,0},{3,27},{4,2},{5,29},{6,4},{7,31},{8,14},{9,1},{... | collective-permute-start | bytes 5898248 | tf_op jit(solution)/shard_map/ppermute | solution.py:33
  89.7 40.6 %collective-permute-start.16 = (bf16[384,1280]{1,0:T(8,128)(2,1)S(1)}, bf16[384,1280]{1,0:T(8,128)(2,1)S(1)}, u32[]{:S(2)}, u32[]{:S(2)}) collective-permute-start(bf16[384,1280]{1,0:T(8,128)(2,1)S(1)} %join.4), channel_id=1, source_target_pairs={{0,2},{1,9},{2,4},{3,11},{4,6},{5,13},{6,0},{7,15},{8,10},{9,17},{... | collective-permute-start | bytes 2949128 | tf_op jit(solution)/shard_map/ppermute | solution.py:33
  89.7 40.6 %collective-permute-start.15 = (bf16[384,1280]{1,0:T(8,128)(2,1)S(1)}, bf16[384,1280]{1,0:T(8,128)(2,1)S(1)}, u32[]{:S(2)}, u32[]{:S(2)}) collective-permute-start(bf16[384,1280]{1,0:T(8,128)(2,1)S(1)} %collective-permute-done.13.refs_0_), channel_id=1, source_target_pairs={{0,8},{1,3},{2,10},{3,5},{4,12},{5,7},{6,14},{7,1},{8,16},{9,11},{... | collective-permute-start | bytes 2949128 | tf_op jit(solution)/shard_map/ppermute | solution.py:33
  119.8 12.2 %collective-permute-start.4 = (bf16[16,48,624]{2,1,0:T(8,128)(2,1)S(1)}, bf16[16,48,624]{2,1,0:T(8,128)(2,1)S(1)}, u32[]{:S(2)}, u32[]{:S(2)}) collective-permute-start(bf16[16,48,624]{2,1,0:T(8,128)(2,1)S(1)} %all_to_all.5.refs_0_), channel_id=1, source_target_pairs={{0,1},{1,0},{2,3},{3,2},{4,5},{5,4},{6,7},{7,6},{8,9},{9,8},{10,11... | collective-permute-start | bytes 2875400 | tf_op jit(solution)/shard_map/ppermute | solution.py:23
  130.3 13.2 %collective-permute-start.17 = (bf16[384,1280]{1,0:T(8,128)(2,1)S(1)}, bf16[384,1280]{1,0:T(8,128)(2,1)S(1)}, u32[]{:S(2)}, u32[]{:S(2)}) collective-permute-start(bf16[384,1280]{1,0:T(8,128)(2,1)S(1)} %join.4), channel_id=1, source_target_pairs={{0,6},{1,25},{2,0},{3,27},{4,2},{5,29},{6,4},{7,31},{8,14},{9,1},{... | collective-permute-start | bytes 2949128 | tf_op jit(solution)/shard_map/ppermute | solution.py:33
  130.3 28.6 %collective-permute-start.20 = (bf16[384,1280]{1,0:T(8,128)(2,1)S(1)}, bf16[384,1280]{1,0:T(8,128)(2,1)S(1)}, u32[]{:S(2)}, u32[]{:S(2)}) collective-permute-start(bf16[384,1280]{1,0:T(8,128)(2,1)S(1)} %collective-permute-done.16), channel_id=1, source_target_pairs={{0,2},{1,9},{2,4},{3,11},{4,6},{5,13},{6,0},{7,15},{8,10},{9,17},{... | collective-permute-start | bytes 2949128 | tf_op jit(solution)/shard_map/ppermute | solution.py:33
  131.8 28.2 %collective-permute-start.21 = (bf16[384,1280]{1,0:T(8,128)(2,1)S(1)}, bf16[384,1280]{1,0:T(8,128)(2,1)S(1)}, u32[]{:S(2)}, u32[]{:S(2)}) collective-permute-start(bf16[384,1280]{1,0:T(8,128)(2,1)S(1)} %collective-permute-done.15), channel_id=1, source_target_pairs={{0,2},{1,9},{2,4},{3,11},{4,6},{5,13},{6,0},{7,15},{8,10},{9,17},{... | collective-permute-start | bytes 2949128 | tf_op jit(solution)/shard_map/ppermute | solution.py:33
  132.0 22.1 %collective-permute-start.22 = (bf16[384,1280]{1,0:T(8,128)(2,1)S(1)}, bf16[384,1280]{1,0:T(8,128)(2,1)S(1)}, u32[]{:S(2)}, u32[]{:S(2)}) collective-permute-start(bf16[384,1280]{1,0:T(8,128)(2,1)S(1)} %collective-permute-done.15), channel_id=1, source_target_pairs={{0,6},{1,25},{2,0},{3,27},{4,2},{5,29},{6,4},{7,31},{8,14},{9,1},{... | collective-permute-start | bytes 2949128 | tf_op jit(solution)/shard_map/ppermute | solution.py:33
  134.6 27.8 %collective-permute-start.23 = (bf16[192,1280]{1,0:T(8,128)(2,1)S(1)}, bf16[192,1280]{1,0:T(8,128)(2,1)S(1)}, u32[]{:S(2)}, u32[]{:S(2)}) collective-permute-start(bf16[192,1280]{1,0:T(8,128)(2,1)S(1)} %slice.18), channel_id=1, source_target_pairs={{0,2},{1,9},{2,4},{3,11},{4,6},{5,13},{6,0},{7,15},{8,10},{9,17},{... | collective-permute-start | bytes 1474568 | tf_op jit(solution)/shard_map/ppermute | solution.py:33
  143.5 26.3 %collective-permute-start.24 = (bf16[576,1280]{1,0:T(8,128)(2,1)S(1)}, bf16[576,1280]{1,0:T(8,128)(2,1)S(1)}, u32[]{:S(2)}, u32[]{:S(2)}) collective-permute-start(bf16[576,1280]{1,0:T(8,128)(2,1)S(1)} %slice.19), channel_id=1, source_target_pairs={{0,6},{1,25},{2,0},{3,27},{4,2},{5,29},{6,4},{7,31},{8,14},{9,1},{... | collective-permute-start | bytes 4423688 | tf_op jit(solution)/shard_map/ppermute | solution.py:33
  154.1 26.3 %collective-permute-start.25 = (bf16[384,1280]{1,0:T(8,128)(2,1)S(1)}, bf16[384,1280]{1,0:T(8,128)(2,1)S(1)}, u32[]{:S(2)}, u32[]{:S(2)}) collective-permute-start(bf16[384,1280]{1,0:T(8,128)(2,1)S(1)} %collective-permute-done.22), channel_id=1, source_target_pairs={{0,6},{1,25},{2,0},{3,27},{4,2},{5,29},{6,4},{7,31},{8,14},{9,1},{... | collective-permute-start | bytes 2949128 | tf_op jit(solution)/shard_map/ppermute | solution.py:33
  181.7 6.2 %collective-permute-start.26 = (f32[312,1280]{1,0:T(8,128)S(1)}, f32[312,1280]{1,0:T(8,128)S(1)}, u32[]{:S(2)}, u32[]{:S(2)}) collective-permute-start(f32[312,1280]{1,0:T(8,128)S(1)} %get-tuple-element.52), channel_id=1, source_target_pairs={{0,1},{1,0},{2,3},{3,2},{4,5},{5,4},{6,7},{7,6},{8,9},{9,8},{10,11... | collective-permute-start | bytes 4792328 | tf_op jit(solution)/shard_map/ppermute | solution.py:23

commit v2 on v1

--- a/solution.py
+++ b/solution.py
@@ -9,7 +9,6 @@
 SIDE = 4
 CORES = 2
 PLANE = SIDE * SIDE
-SOURCES = CORES * SIDE
 WIDE = 1280
 VMEM = pl.BlockSpec(memory_space=pltpu.VMEM)
 SMEM = pl.BlockSpec(memory_space=pltpu.SMEM)
@@ -55,7 +54,7 @@
 
 
 def pack_kernel(count_ref, terms_ref, *refs):
-    window_refs, rows_ref, windows = refs[:SOURCES], refs[-2], refs[-1]
+    mine_refs, theirs_ref, rows_ref, windows = refs[:SIDE], refs[-3], refs[-2], refs[-1]
     slots, orbitals, basis = terms_ref.shape
     columns = basis // SIDE
     chip_rows = rows_ref.shape[2]
@@ -74,48 +73,71 @@
         for i in range(PLANE):
             block = terms_ref[s, :, i * chip_rows : (i + 1) * chip_rows]
             rows_ref[i, at, :] = jnp.where(live, block, jnp.zeros_like(block))
-    for dcore in range(CORES):
-        for dy in range(SIDE):
-            to = lax.rem(y + dy, SIDE) * CORES + lax.rem(core + dcore, CORES)
-            window_refs[dcore * SIDE + dy][...] = windows[to]
+    for dy in range(SIDE):
+        plane = lax.rem(y + dy, SIDE) * CORES
+        mine_refs[dy][...] = windows[plane + core]
+        theirs_ref[dy] = windows[plane + 1 - core]
 
 
 def pack(counts, terms):
     slots, orbitals, basis = terms.shape
     depth = slots * orbitals
     window = jax.ShapeDtypeStruct((depth, WIDE), terms.dtype)
+    other_windows = jax.ShapeDtypeStruct((SIDE, depth, WIDE), terms.dtype)
     chip_rows = jax.ShapeDtypeStruct((PLANE, depth, basis // PLANE), terms.dtype)
-    *windows, rows = pl.pallas_call(
+    *mine, theirs, rows = pl.pallas_call(
         pack_kernel,
-        out_shape=(window,) * SOURCES + (chip_rows,),
+        out_shape=(window,) * SIDE + (other_windows, chip_rows),
         in_specs=[SMEM, VMEM],
-        out_specs=(VMEM,) * (SOURCES + 1),
-        scratch_shapes=[pltpu.VMEM((SOURCES, depth, WIDE), terms.dtype)],
+        out_specs=(VMEM,) * (SIDE + 2),
+        scratch_shapes=[pltpu.VMEM((CORES * SIDE, depth, WIDE), terms.dtype)],
         compiler_params=pltpu.CompilerParams(vmem_limit_bytes=10 << 20),
         name="pack",
     )(counts, terms)
-    return windows, rows
-
-
-def exchanged(windows):
-    from_offset = {}
-    for dcore in range(CORES):
-        for dy in (2, 1, 3, 0):
-            block = windows[dcore * SIDE + dy]
-            if dy or dcore:
-                route = [
-                    (y * CORES + core, (y + dy) % SIDE * CORES + (core + dcore) % CORES)
-                    for y in range(SIDE)
-                    for core in range(CORES)
-                ]
-                block = lax.ppermute(block, ("y", "core"), route)
-            from_offset[dcore, -dy % SIDE] = block
-    return join([from_offset[dcore, dy] for dcore in range(CORES) for dy in range(SIDE)])
+    return mine, theirs, rows
+
+
+def pair_kernel(*refs):
+    mine_refs, got_ref, out_refs = refs[:SIDE], refs[SIDE], refs[SIDE + 1 :]
+    depth = got_ref.shape[1]
+    for dy in range(SIDE):
+        out_refs[dy][:depth, :] = mine_refs[dy][...]
+        out_refs[dy][depth:, :] = got_ref[dy]
+
+
+def pair(mine, got):
+    window = jax.ShapeDtypeStruct((CORES * got.shape[1], WIDE), got.dtype)
+    return pl.pallas_call(
+        pair_kernel,
+        out_shape=(window,) * SIDE,
+        in_specs=[VMEM] * (SIDE + 1),
+        out_specs=(VMEM,) * SIDE,
+        compiler_params=pltpu.CompilerParams(vmem_limit_bytes=6 << 20),
+        name="pair",
+    )(*mine, got)
+
+
+OWN = tuple((dcore, 0) for dcore in range(CORES))
+OTHERS = tuple((dcore, dy) for dy in range(1, SIDE) for dcore in range(CORES))
+
+
+def at(v, *us):
+    return tuple((u, v) for u in us)
+
+
+def gathered_briefly(own):
+    before, after = along_plane(own, 0, 1), along_plane(own, 0, -1)
+    far = along_plane(before, 0, 1)
+    line = join([own, before, after, far])
+    left, right = along_plane(line, 1, 1), along_plane(line, 1, -1)
+    cut = line.shape[0] // 2
+    opposite = along_plane(left[:cut], 1, 1), along_plane(right[cut:], 1, -1)
+    offsets = at(0, 0, -1, 1, 2) + at(-1, 0, -1, 1, 2) + at(1, 0, -1, 1, 2) + at(2, 0, -1, 1, 2)
+    return offsets, (line, left, right, *opposite)
 
 
 def gathered(own):
-    depth = own.shape[0]
-    cut = depth // 2
+    cut = own.shape[0] // 2
     before, after = along_plane(own, 0, 1), along_plane(own, 0, -1)
     near = join([before, after])
     own_sides = along_plane(own, 1, 1), along_plane(own, 1, -1)
@@ -126,44 +148,39 @@
     near_opposite = along_plane(near_sides[0][:cut], 1, 1), along_plane(near_sides[1][cut:], 1, -1)
     far_opposite = along_plane(far_sides[1], 1, -1)
 
-    def at(v, *us):
-        return tuple((u, v) for u in us)
-
     parts = [(at(0, 0), 0, own), (at(0, -1, 1), 0, near), (at(0, 2), 0, far)]
     parts += [(at(v, 0), 0, block) for v, block in zip((-1, 1), own_sides)]
     parts += [(at(v, -1, 1), 0, block) for v, block in zip((-1, 1), near_sides)]
     parts += [(at(2, 0), 0, own_opposite)]
     parts += [(at(v, 2), 0, block) for v, block in zip((-1, 1), far_sides)]
-    parts += [(at(2, -1, 1), 0, near_opposite[0]), (at(2, -1, 1), SOURCES // 2, near_opposite[1])]
+    parts += [(at(2, -1, 1), 0, near_opposite[0]), (at(2, -1, 1), len(OTHERS) // 2, near_opposite[1])]
     parts += [(at(2, 2), 0, far_opposite)]
     return parts
 
 
-def arrange_kernel(layout, rows_ref, rest_ref, other_rows_ref, other_rest_ref, *out_refs):
-    depth = rows_ref.shape[1]
+def arrange_kernel(layout, *refs):
+    in_refs, out_refs = refs[: -len(layout)], refs[-len(layout) :]
+    depth = in_refs[0].shape[1]
     x, z, core = (lax.axis_index(name) for name in ("x", "z", "core"))
     for blocks, out_ref in zip(layout, out_refs):
-        for i, (u, v, source) in enumerate(blocks):
+        for i, (u, v, dcore, place) in enumerate(blocks):
             dx, dz = jnp.where(core == 0, u, v), jnp.where(core == 0, v, u)
             chip = lax.rem(x + dx + SIDE, SIDE) * SIDE + lax.rem(z + dz + SIDE, SIDE)
-            dcore, dy = divmod(source, SIDE)
-            if dy == 0:
-                block = (rows_ref, other_rows_ref)[dcore][chip]
-            else:
-                block = (rest_ref, other_rest_ref)[dcore][(dy - 1) * PLANE + chip]
-            out_ref[i * depth : (i + 1) * depth, :] = block
-
-
-def arrange(layout, rows, rest, other_rows, other_rest):
-    depth, chip_rows = rows.shape[1:]
+            out_ref[i * depth : (i + 1) * depth, :] = in_refs[dcore][place * PLANE + chip]
+
+
+def arrange(layout, *rows):
+    depth, chip_rows = rows[0].shape[1:]
+    size = sum(map(len, layout)) * depth * chip_rows * rows[0].dtype.itemsize
     return pl.pallas_call(
         lambda *refs: arrange_kernel(layout, *refs),
-        out_shape=tuple(jax.ShapeDtypeStruct((len(blocks) * depth, chip_rows), rows.dtype) for blocks in layout),
-        in_specs=[VMEM] * 4,
+        out_shape=tuple(jax.ShapeDtypeStruct((len(blocks) * depth, chip_rows), rows[0].dtype) for blocks in layout),
+        in_specs=[VMEM] * CORES,
         out_specs=(VMEM,) * len(layout),
-        compiler_params=pltpu.CompilerParams(vmem_limit_bytes=16 << 20),
+        compiler_params=pltpu.CompilerParams(vmem_limit_bytes=2 * size + (1 << 20)),
+        cost_estimate=pl.CostEstimate(flops=0, bytes_accessed=2 * size, transcendentals=0),
         name="arrange",
-    )(rows, rest, other_rows, other_rest)
+    )(*rows)
 
 
 def halve_kernel(tile_ref, kept_ref, sent_ref):
@@ -212,11 +229,14 @@
 
 def body(b_tensor, aux_counts):
     basis = b_tensor.shape[0]
-    windows, rows = pack(aux_counts, b_tensor.transpose(1, 2, 0))
-
-    columns = exchanged(windows)
+    mine, theirs, rows = pack(aux_counts, b_tensor.transpose(1, 2, 0))
+
+    got = swap_cores(theirs)
+    windows = pair(mine, got)
+    others = join([along_y(windows[-dy % SIDE], -dy % SIDE) for dy in range(1, SIDE)])
     rows = lax.all_to_all(rows, ("x", "z"), 0, 0, tiled=True)
-    parts = gathered(columns)
+    offsets, early = gathered_briefly(windows[0])
+    parts = gathered(others)
 
     left, right = along_y(rows, 1), along_y(rows, -1)
     half = PLANE // 2
@@ -225,16 +245,18 @@
     other_rows = swap_cores(rows)
     other_rest = swap_cores(rest)
 
+    def product(weight, block):
+        return lax.dot_general(weight, block, (((0,), (0,)), ((), ())), preferred_element_type=jnp.float32)
+
+    (weight,) = arrange([[(u, v, dcore, dy) for u, v in offsets for dcore, dy in OWN]], rows, other_rows)
+    tile = product(weight, join(early))
     layout = []
     for offsets, skipped, block in parts:
-        blocks = [(u, v, source) for u, v in offsets for source in range(SOURCES)]
+        blocks = [(u, v, dcore, dy - 1) for u, v in offsets for dcore, dy in OTHERS]
         layout.append(blocks[skipped : skipped + block.shape[0] // rows.shape[1]])
-    weights = arrange(layout, rows, rest, other_rows, other_rest)
-
-    tile = None
+    weights = arrange(layout, rest, other_rest)
     for (_, _, block), weight in zip(parts, weights):
-        product = lax.dot_general(weight, block, (((0,), (0,)), ((), ())), preferred_element_type=jnp.float32)
-        tile = lax.optimization_barrier(product if tile is None else tile + product)
+        tile = lax.optimization_barrier(tile + product(weight, block))
 
     kept, sent = halve(tile)
     return assemble(kept, swap_cores(sent), basis // SIDE)

time: 190 us -> 213 us (1.12); the launches traced: 190 us -> 209 us
  starting transfers between devices: 36.4 us -> 62.3 us
  waiting for transfers between devices: 106 us -> 95.4 us
  matrix products: 14.6 us -> 17.1 us
    ppermute x4 -> x7, waiting for transfers between devices: 1.04 us -> 32.9 us  [along_y(): lax.ppermute(block, 'y', [(i, (i + step) % SIDE) for i in range(SIDE)])]
    ppermute x3 -> x4, starting transfers between devices: 7.43 us -> 36.2 us  [swap_cores(): return lax.ppermute(block, 'core', [(0, 1), (1, 0)])]
    ppermute x7 -> x0, waiting for transfers between devices: 28.6 us -> none  [exchanged(): block = lax.ppermute(block, ('y', 'core'), route)]
    ppermute x13 -> x20, waiting for transfers between devices: 73 us -> 59.5 us  [along_plane(): return lax.ppermute(block, ('x', 'z', 'core'), route)]
    ppermute x7 -> x0, starting transfers between devices: 11.7 us -> none  [exchanged(): block = lax.ppermute(block, ('y', 'core'), route)]
    ppermute x13 -> x20, starting transfers between devices: 11.7 us -> 19 us  [along_plane(): return lax.ppermute(block, ('x', 'z', 'core'), route)]
    dot_general x13 -> x14, matrix products: 14.6 us -> 17.1 us  [product(): lax.dot_general(weight, block, (((0,), (0,)), ((), ())), preferred_elemen...]
    ppermute x4 -> x7, starting transfers between devices: 5.53 us -> 7.07 us  [along_y(): lax.ppermute(block, 'y', [(i, (i + step) % SIDE) for i in range(SIDE)])]
  transfers between devices with their start and end apart: 27 -> 31, of which waited for: 13 -> 14; matrix products, arithmetic and copies ran while one was open for 9% -> 9% of each run, Pallas kernels for 1% -> 1%
where the time goes in v2:
time: 213 us; the launch traced here: 209 us
  waiting for transfers between devices  95.4 us (45%)
  starting transfers between devices  62.3 us (29%)
  blocking collectives  23.5 us (11%)
  matrix products  17.1 us (8%)
  Pallas kernels  4.61 us (2%)
  other arithmetic  3.28 us (2%)
    ppermute x20, waiting for transfers between devices, along_plane(): return lax.ppermute(block, ('x', 'z', 'core'), route)  59.5 us
    ppermute x4, starting transfers between devices, swap_cores(): return lax.ppermute(block, 'core', [(0, 1), (1, 0)])  36.2 us
    ppermute x7, waiting for transfers between devices, along_y(): lax.ppermute(block, 'y', [(i, (i + step) % SIDE) for i in range(SIDE)])  32.9 us
    all_to_all x1, blocking collectives, body(): rows = lax.all_to_all(rows, ('x', 'z'), 0, 0, tiled=True)  23.5 us
    ppermute x20, starting transfers between devices, along_plane(): return lax.ppermute(block, ('x', 'z', 'core'), route)  19 us
    dot_general x14, matrix products, product(): lax.dot_general(weight, block, (((0,), (0,)), ((), ())), preferred_elemen...  17.1 us
    ppermute x7, starting transfers between devices, along_y(): lax.ppermute(block, 'y', [(i, (i + step) % SIDE) for i in range(SIDE)])  7.07 us
  transfers between devices with their start and end apart: 31, of which 14 were waited for; matrix products, arithmetic and copies ran while one was open for 9% of the time, Pallas kernels for 1%

profile of v2, /device:TPU:1, one launch (start us, length us, event | category | flops | bytes accessed | tf_op | source)
XLA Modules:
  0.0 208.6 jit_solution(9351426675037277721)
XLA Ops:
  3.0 23.5 %all_to_all.5.refs_0_ = bf16[16,48,624]{2,1,0:T(8,128)(2,1)S(1)} all-to-all(bf16[16,48,624]{2,1,0:T(8,128)(2,1)S(1)} %get-tuple-element.30), channel_id=1, replica_groups=mesh['y'=4,'x'=4,'z'=4,'core'=2] {'x','z'}, dimensions={0} | all-to-all | bytes 1916928 | tf_op jit(solution)/shard_map/all_to_all | solution.py:237
  27.8 1.4 collective-permute-start.9
  29.2 2.3 %collective-permute-start.1 = (bf16[4,48,1280]{2,1,0:T(8,128)(2,1)S(1)}, bf16[4,48,1280]{2,1,0:T(8,128)(2,1)S(1)}, u32[]{:S(2)}, u32[]{:S(2)}) collective-permute-start(bf16[4,48,1280]{2,1,0:T(8,128)(2,1)S(1)} %get-tuple-element.35), channel_id=1, source_target_pairs={{0,1},{1,0},{2,3},{3,2},{4,5},{5,4},{6,7},{7,6},{8,9},{9,8},{10,11... | collective-permute-start | bytes 1474568 | tf_op jit(solution)/shard_map/ppermute | solution.py:22
  31.5 17.8 %collective-permute-done.10.refs_3_ = bf16[16,48,624]{2,1,0:T(8,128)(2,1)S(1)} collective-permute-done((bf16[16,48,624]{2,1,0:T(8,128)(2,1)S(1)}, bf16[16,48,624]{2,1,0:T(8,128)(2,1)S(1)}, u32[]{:S(2)}, u32[]{:S(2)}) %collective-permute-start.10) | collective-permute-done | bytes 958496 | tf_op jit(solution)/shard_map/ppermute | solution.py:18
  49.5 2.7 %collective-permute-start.12 = (bf16[8,48,624]{2,1,0:T(8,128)(2,1)S(1)}, bf16[8,48,624]{2,1,0:T(8,128)(2,1)S(1)}, u32[]{:S(2)}, u32[]{:S(2)}) collective-permute-start(bf16[8,48,624]{2,1,0:T(8,128)(2,1)S(1)} %slice.27), channel_id=1, source_target_pairs={{0,96},{32,0},{64,32},{96,64},{1,97},{33,1},{65,33},{97,65},{2,98}... | collective-permute-start | bytes 1437704 | tf_op jit(solution)/shard_map/ppermute | solution.py:18
  53.8 12.3 %collective-permute-done.14.refs_0_ = bf16[96,1280]{1,0:T(8,128)(2,1)S(1)} collective-permute-done((bf16[96,1280]{1,0:T(8,128)(2,1)S(1)}, bf16[96,1280]{1,0:T(8,128)(2,1)S(1)}, u32[]{:S(2)}, u32[]{:S(2)}) %collective-permute-start.14) | collective-permute-done | bytes 245792 | tf_op jit(solution)/shard_map/ppermute | solution.py:18
  66.1 1.6 collective-permute-start.2
  67.7 2.8 %collective-permute-done.16.refs_2_ = bf16[96,1280]{1,0:T(8,128)(2,1)S(1)} collective-permute-done((bf16[96,1280]{1,0:T(8,128)(2,1)S(1)}, bf16[96,1280]{1,0:T(8,128)(2,1)S(1)}, u32[]{:S(2)}, u32[]{:S(2)}) %collective-permute-start.16) | collective-permute-done | bytes 245792 | tf_op jit(solution)/shard_map/ppermute | solution.py:18
  70.5 2.5 %collective-permute-start.17 = (bf16[288,1280]{1,0:T(8,128)(2,1)S(1)}, bf16[288,1280]{1,0:T(8,128)(2,1)S(1)}, u32[]{:S(2)}, u32[]{:S(2)}) collective-permute-start(bf16[288,1280]{1,0:T(8,128)(2,1)S(1)} %join.8), channel_id=1, source_target_pairs={{0,8},{1,3},{2,10},{3,5},{4,12},{5,7},{6,14},{7,1},{8,16},{9,11},{... | collective-permute-start | bytes 2211848 | tf_op jit(solution)/shard_map/ppermute | solution.py:32
  73.3 2.4 %collective-permute-start.13 = (bf16[48,48,624]{2,1,0:T(8,128)(2,1)S(1)}, bf16[48,48,624]{2,1,0:T(8,128)(2,1)S(1)}, u32[]{:S(2)}, u32[]{:S(2)}) collective-permute-start(bf16[48,48,624]{2,1,0:T(8,128)(2,1)S(1)} %join.7.refs_0_), channel_id=1, source_target_pairs={{0,1},{1,0},{2,3},{3,2},{4,5},{5,4},{6,7},{7,6},{8,9},{9,8},{10,11... | collective-permute-start | bytes 8626184 | tf_op jit(solution)/shard_map/ppermute | solution.py:22
  77.1 3.9 %collective-permute-done.3.refs_2_ = bf16[96,1280]{1,0:T(8,128)(2,1)S(1)} collective-permute-done((bf16[96,1280]{1,0:T(8,128)(2,1)S(1)}, bf16[96,1280]{1,0:T(8,128)(2,1)S(1)}, u32[]{:S(2)}, u32[]{:S(2)}) %collective-permute-start.3) | collective-permute-done | bytes 245792 | tf_op jit(solution)/shard_map/ppermute | solution.py:32
  81.0 4.0 %collective-permute-done.4.refs_3_ = bf16[96,1280]{1,0:T(8,128)(2,1)S(1)} collective-permute-done((bf16[96,1280]{1,0:T(8,128)(2,1)S(1)}, bf16[96,1280]{1,0:T(8,128)(2,1)S(1)}, u32[]{:S(2)}, u32[]{:S(2)}) %collective-permute-start.4) | collective-permute-done | bytes 245792 | tf_op jit(solution)/shard_map/ppermute | solution.py:32
  85.2 2.7 %collective-permute-start.6 = (bf16[384,1280]{1,0:T(8,128)(2,1)S(1)}, bf16[384,1280]{1,0:T(8,128)(2,1)S(1)}, u32[]{:S(2)}, u32[]{:S(2)}) collective-permute-start(bf16[384,1280]{1,0:T(8,128)(2,1)S(1)} %join.5.refs_0_), channel_id=1, source_target_pairs={{0,6},{1,25},{2,0},{3,27},{4,2},{5,29},{6,4},{7,31},{8,14},{9,1},{... | collective-permute-start | bytes 2949128 | tf_op jit(solution)/shard_map/ppermute | solution.py:32
  87.9 10.5 %collective-permute-start = (bf16[16,48,624]{2,1,0:T(8,128)(2,1)S(1)}, bf16[16,48,624]{2,1,0:T(8,128)(2,1)S(1)}, u32[]{:S(2)}, u32[]{:S(2)}) collective-permute-start(bf16[16,48,624]{2,1,0:T(8,128)(2,1)S(1)} %all_to_all.5.refs_0_), channel_id=1, source_target_pairs={{0,1},{1,0},{2,3},{3,2},{4,5},{5,4},{6,7},{7,6},{8,9},{9,8},{10,11... | collective-permute-start | bytes 2875400 | tf_op jit(solution)/shard_map/ppermute | solution.py:22
  98.5 1.6 collective-permute-start.22
  100.0 2.2 %collective-permute-done.5.refs_1_ = bf16[384,1280]{1,0:T(8,128)(2,1)S(1)} collective-permute-done((bf16[384,1280]{1,0:T(8,128)(2,1)S(1)}, bf16[384,1280]{1,0:T(8,128)(2,1)S(1)}, u32[]{:S(2)}, u32[]{:S(2)}) %collective-permute-start.5) | collective-permute-done | bytes 983072 | tf_op jit(solution)/shard_map/ppermute | solution.py:32
  102.3 1.5 collective-permute-start.7
  105.2 18.3 %collective-permute-done.7.refs_3_ = bf16[192,1280]{1,0:T(8,128)(2,1)S(1)} collective-permute-done((bf16[192,1280]{1,0:T(8,128)(2,1)S(1)}, bf16[192,1280]{1,0:T(8,128)(2,1)S(1)}, u32[]{:S(2)}, u32[]{:S(2)}) %collective-permute-start.7) | collective-permute-done | bytes 491552 | tf_op jit(solution)/shard_map/ppermute | solution.py:32
  123.8 6.4 %collective-permute-done.8.refs_4_ = bf16[192,1280]{1,0:T(8,128)(2,1)S(1)} collective-permute-done((bf16[192,1280]{1,0:T(8,128)(2,1)S(1)}, bf16[192,1280]{1,0:T(8,128)(2,1)S(1)}, u32[]{:S(2)}, u32[]{:S(2)}) %collective-permute-start.8) | collective-permute-done | bytes 491552 | tf_op jit(solution)/shard_map/ppermute | solution.py:32
  130.7 4.7 %collective-permute-done.20 = bf16[288,1280]{1,0:T(8,128)(2,1)S(1)} collective-permute-done((bf16[288,1280]{1,0:T(8,128)(2,1)S(1)}, bf16[288,1280]{1,0:T(8,128)(2,1)S(1)}, u32[]{:S(2)}, u32[]{:S(2)}) %collective-permute-start.20) | collective-permute-done | bytes 737312 | tf_op jit(solution)/shard_map/ppermute | solution.py:32
  135.3 11.6 %collective-permute-done.19 = bf16[288,1280]{1,0:T(8,128)(2,1)S(1)} collective-permute-done((bf16[288,1280]{1,0:T(8,128)(2,1)S(1)}, bf16[288,1280]{1,0:T(8,128)(2,1)S(1)}, u32[]{:S(2)}, u32[]{:S(2)}) %collective-permute-start.19) | collective-permute-done | bytes 737312 | tf_op jit(solution)/shard_map/ppermute | solution.py:32
  147.0 2.7 %collective-permute-start.26 = (bf16[288,1280]{1,0:T(8,128)(2,1)S(1)}, bf16[288,1280]{1,0:T(8,128)(2,1)S(1)}, u32[]{:S(2)}, u32[]{:S(2)}) collective-permute-start(bf16[288,1280]{1,0:T(8,128)(2,1)S(1)} %collective-permute-done.19), channel_id=1, source_target_pairs={{0,6},{1,25},{2,0},{3,27},{4,2},{5,29},{6,4},{7,31},{8,14},{9,1},{... | collective-permute-start | bytes 2211848 | tf_op jit(solution)/shard_map/ppermute | solution.py:32
  151.6 2.8 %convolution_add_fusion.4 = f32[624,1280]{1,0:T(8,128)S(1)} fusion(f32[624,1280]{1,0:T(8,128)S(1)} %fusion, bf16[1536,624]{1,0:T(8,128)(2,1)S(1)} %arrange.2, bf16[1536,1280]{1,0:T(8,128)(2,1)S(1)} %join.6), kind=kOutput, calls=%fused_computation.4 | convolution fusion | flops 2454466560 | bytes 12238848 | tf_op jit(solution)/shard_map/dot_general | solution.py:249
  154.5 1.4 fusion.1
  158.4 2.7 %collective-permute-start.28 = (bf16[432,1280]{1,0:T(8,128)(2,1)S(1)}, bf16[432,1280]{1,0:T(8,128)(2,1)S(1)}, u32[]{:S(2)}, u32[]{:S(2)}) collective-permute-start(bf16[432,1280]{1,0:T(8,128)(2,1)S(1)} %slice.29), channel_id=1, source_target_pairs={{0,6},{1,25},{2,0},{3,27},{4,2},{5,29},{6,4},{7,31},{8,14},{9,1},{... | collective-permute-start | bytes 3317768 | tf_op jit(solution)/shard_map/ppermute | solution.py:32
  163.3 1.4 fusion.4
  165.1 1.4 fusion.5
  168.1 5.0 %collective-permute-done.25 = bf16[288,1280]{1,0:T(8,128)(2,1)S(1)} collective-permute-done((bf16[288,1280]{1,0:T(8,128)(2,1)S(1)}, bf16[288,1280]{1,0:T(8,128)(2,1)S(1)}, u32[]{:S(2)}, u32[]{:S(2)}) %collective-permute-start.25) | collective-permute-done | bytes 737312 | tf_op jit(solution)/shard_map/ppermute | solution.py:32
  179.6 1.8 collective-permute-done.29
  182.6 21.0 %collective-permute-start.30 = (f32[312,1280]{1,0:T(8,128)S(1)}, f32[312,1280]{1,0:T(8,128)S(1)}, u32[]{:S(2)}, u32[]{:S(2)}) collective-permute-start(f32[312,1280]{1,0:T(8,128)S(1)} %get-tuple-element.54), channel_id=1, source_target_pairs={{0,1},{1,0},{2,3},{3,2},{4,5},{5,4},{6,7},{7,6},{8,9},{9,8},{10,11... | collective-permute-start | bytes 4792328 | tf_op jit(solution)/shard_map/ppermute | solution.py:22
  203.7 3.1 %collective-permute-done.30.got_ref = f32[312,1280]{1,0:T(8,128)S(1)} collective-permute-done((f32[312,1280]{1,0:T(8,128)S(1)}, f32[312,1280]{1,0:T(8,128)S(1)}, u32[]{:S(2)}, u32[]{:S(2)}) %collective-permute-start.30) | collective-permute-done | bytes 1597472 | tf_op jit(solution)/shard_map/ppermute | solution.py:22
  206.7 1.9 assemble.1
  (74 shorter events, 26.1 us)
Async XLA Ops:
  0.0 1.2 copy-start
  26.5 22.8 %collective-permute-start.10 = (bf16[16,48,624]{2,1,0:T(8,128)(2,1)S(1)}, bf16[16,48,624]{2,1,0:T(8,128)(2,1)S(1)}, u32[]{:S(2)}, u32[]{:S(2)}) collective-permute-start(bf16[16,48,624]{2,1,0:T(8,128)(2,1)S(1)} %all_to_all.5.refs_0_), channel_id=1, source_target_pairs={{0,32},{32,64},{64,96},{96,0},{1,33},{33,65},{65,97},{97,1},{2,34}... | collective-permute-start | bytes 2875400 | tf_op jit(solution)/shard_map/ppermute | solution.py:18
  27.8 21.7 %collective-permute-start.9 = (bf16[16,48,624]{2,1,0:T(8,128)(2,1)S(1)}, bf16[16,48,624]{2,1,0:T(8,128)(2,1)S(1)}, u32[]{:S(2)}, u32[]{:S(2)}) collective-permute-start(bf16[16,48,624]{2,1,0:T(8,128)(2,1)S(1)} %all_to_all.5.refs_0_), channel_id=1, source_target_pairs={{0,96},{32,0},{64,32},{96,64},{1,97},{33,1},{65,33},{97,65},{2,98}... | collective-permute-start | bytes 2875400 | tf_op jit(solution)/shard_map/ppermute | solution.py:18
  29.2 23.0 %collective-permute-start.1 = (bf16[4,48,1280]{2,1,0:T(8,128)(2,1)S(1)}, bf16[4,48,1280]{2,1,0:T(8,128)(2,1)S(1)}, u32[]{:S(2)}, u32[]{:S(2)}) collective-permute-start(bf16[4,48,1280]{2,1,0:T(8,128)(2,1)S(1)} %get-tuple-element.35), channel_id=1, source_target_pairs={{0,1},{1,0},{2,3},{3,2},{4,5},{5,4},{6,7},{7,6},{8,9},{9,8},{10,11... | collective-permute-start | bytes 1474568 | tf_op jit(solution)/shard_map/ppermute | solution.py:22
  49.3 23.7 %collective-permute-start.11 = (bf16[8,48,624]{2,1,0:T(8,128)(2,1)S(1)}, bf16[8,48,624]{2,1,0:T(8,128)(2,1)S(1)}, u32[]{:S(2)}, u32[]{:S(2)}) collective-permute-start(bf16[8,48,624]{2,1,0:T(8,128)(2,1)S(1)} %slice.26), channel_id=1, source_target_pairs={{0,32},{32,64},{64,96},{96,0},{1,33},{33,65},{65,97},{97,1},{2,34}... | collective-permute-start | bytes 1437704 | tf_op jit(solution)/shard_map/ppermute | solution.py:18
  49.5 23.5 %collective-permute-start.12 = (bf16[8,48,624]{2,1,0:T(8,128)(2,1)S(1)}, bf16[8,48,624]{2,1,0:T(8,128)(2,1)S(1)}, u32[]{:S(2)}, u32[]{:S(2)}) collective-permute-start(bf16[8,48,624]{2,1,0:T(8,128)(2,1)S(1)} %slice.27), channel_id=1, source_target_pairs={{0,96},{32,0},{64,32},{96,64},{1,97},{33,1},{65,33},{97,65},{2,98}... | collective-permute-start | bytes 1437704 | tf_op jit(solution)/shard_map/ppermute | solution.py:18
  52.3 13.8 %collective-permute-start.14 = (bf16[96,1280]{1,0:T(8,128)(2,1)S(1)}, bf16[96,1280]{1,0:T(8,128)(2,1)S(1)}, u32[]{:S(2)}, u32[]{:S(2)}) collective-permute-start(bf16[96,1280]{1,0:T(8,128)(2,1)S(1)} %get-tuple-element.38), channel_id=1, source_target_pairs={{0,96},{32,0},{64,32},{96,64},{1,97},{33,1},{65,33},{97,65},{2,98}... | collective-permute-start | bytes 737288 | tf_op jit(solution)/shard_map/ppermute | solution.py:18
  52.5 15.2 %collective-permute-start.15 = (bf16[96,1280]{1,0:T(8,128)(2,1)S(1)}, bf16[96,1280]{1,0:T(8,128)(2,1)S(1)}, u32[]{:S(2)}, u32[]{:S(2)}) collective-permute-start(bf16[96,1280]{1,0:T(8,128)(2,1)S(1)} %get-tuple-element.39), channel_id=1, source_target_pairs={{0,64},{32,96},{64,0},{96,32},{1,65},{33,97},{65,1},{97,33},{2,66}... | collective-permute-start | bytes 737288 | tf_op jit(solution)/shard_map/ppermute | solution.py:18
  52.9 17.5 %collective-permute-start.16 = (bf16[96,1280]{1,0:T(8,128)(2,1)S(1)}, bf16[96,1280]{1,0:T(8,128)(2,1)S(1)}, u32[]{:S(2)}, u32[]{:S(2)}) collective-permute-start(bf16[96,1280]{1,0:T(8,128)(2,1)S(1)} %get-tuple-element.40), channel_id=1, source_target_pairs={{0,32},{32,64},{64,96},{96,0},{1,33},{33,65},{65,97},{97,1},{2,34}... | collective-permute-start | bytes 737288 | tf_op jit(solution)/shard_map/ppermute | solution.py:18
  66.1 10.7 %collective-permute-start.2 = (bf16[96,1280]{1,0:T(8,128)(2,1)S(1)}, bf16[96,1280]{1,0:T(8,128)(2,1)S(1)}, u32[]{:S(2)}, u32[]{:S(2)}) collective-permute-start(bf16[96,1280]{1,0:T(8,128)(2,1)S(1)} %get-tuple-element.36.refs_0_), channel_id=1, source_target_pairs={{0,8},{1,3},{2,10},{3,5},{4,12},{5,7},{6,14},{7,1},{8,16},{9,11},{... | collective-permute-start | bytes 737288 | tf_op jit(solution)/shard_map/ppermute | solution.py:32
  70.5 17.3 %collective-permute-start.17 = (bf16[288,1280]{1,0:T(8,128)(2,1)S(1)}, bf16[288,1280]{1,0:T(8,128)(2,1)S(1)}, u32[]{:S(2)}, u32[]{:S(2)}) collective-permute-start(bf16[288,1280]{1,0:T(8,128)(2,1)S(1)} %join.8), channel_id=1, source_target_pairs={{0,8},{1,3},{2,10},{3,5},{4,12},{5,7},{6,14},{7,1},{8,16},{9,11},{... | collective-permute-start | bytes 2211848 | tf_op jit(solution)/shard_map/ppermute | solution.py:32
  73.3 76.6 %collective-permute-start.13 = (bf16[48,48,624]{2,1,0:T(8,128)(2,1)S(1)}, bf16[48,48,624]{2,1,0:T(8,128)(2,1)S(1)}, u32[]{:S(2)}, u32[]{:S(2)}) collective-permute-start(bf16[48,48,624]{2,1,0:T(8,128)(2,1)S(1)} %join.7.refs_0_), channel_id=1, source_target_pairs={{0,1},{1,0},{2,3},{3,2},{4,5},{5,4},{6,7},{7,6},{8,9},{9,8},{10,11... | collective-permute-start | bytes 8626184 | tf_op jit(solution)/shard_map/ppermute | solution.py:22
  75.7 5.3 %collective-permute-start.3 = (bf16[96,1280]{1,0:T(8,128)(2,1)S(1)}, bf16[96,1280]{1,0:T(8,128)(2,1)S(1)}, u32[]{:S(2)}, u32[]{:S(2)}) collective-permute-start(bf16[96,1280]{1,0:T(8,128)(2,1)S(1)} %get-tuple-element.36.refs_0_), channel_id=1, source_target_pairs={{0,24},{1,7},{2,26},{3,1},{4,28},{5,3},{6,30},{7,5},{8,0},{9,15},{... | collective-permute-start | bytes 737288 | tf_op jit(solution)/shard_map/ppermute | solution.py:32
  76.9 8.2 %collective-permute-start.4 = (bf16[96,1280]{1,0:T(8,128)(2,1)S(1)}, bf16[96,1280]{1,0:T(8,128)(2,1)S(1)}, u32[]{:S(2)}, u32[]{:S(2)}) collective-permute-start(bf16[96,1280]{1,0:T(8,128)(2,1)S(1)} %collective-permute-done.2.refs_1_), channel_id=1, source_target_pairs={{0,8},{1,3},{2,10},{3,5},{4,12},{5,7},{6,14},{7,1},{8,16},{9,11},{... | collective-permute-start | bytes 737288 | tf_op jit(solution)/shard_map/ppermute | solution.py:32
  85.1 17.1 %collective-permute-start.5 = (bf16[384,1280]{1,0:T(8,128)(2,1)S(1)}, bf16[384,1280]{1,0:T(8,128)(2,1)S(1)}, u32[]{:S(2)}, u32[]{:S(2)}) collective-permute-start(bf16[384,1280]{1,0:T(8,128)(2,1)S(1)} %join.5.refs_0_), channel_id=1, source_target_pairs={{0,2},{1,9},{2,4},{3,11},{4,6},{5,13},{6,0},{7,15},{8,10},{9,17},{... | collective-permute-start | bytes 2949128 | tf_op jit(solution)/shard_map/ppermute | solution.py:32
  85.2 17.1 %collective-permute-start.6 = (bf16[384,1280]{1,0:T(8,128)(2,1)S(1)}, bf16[384,1280]{1,0:T(8,128)(2,1)S(1)}, u32[]{:S(2)}, u32[]{:S(2)}) collective-permute-start(bf16[384,1280]{1,0:T(8,128)(2,1)S(1)} %join.5.refs_0_), channel_id=1, source_target_pairs={{0,6},{1,25},{2,0},{3,27},{4,2},{5,29},{6,4},{7,31},{8,14},{9,1},{... | collective-permute-start | bytes 2949128 | tf_op jit(solution)/shard_map/ppermute | solution.py:32
  87.9 10.5 %collective-permute-start.18 = (bf16[288,1280]{1,0:T(8,128)(2,1)S(1)}, bf16[288,1280]{1,0:T(8,128)(2,1)S(1)}, u32[]{:S(2)}, u32[]{:S(2)}) collective-permute-start(bf16[288,1280]{1,0:T(8,128)(2,1)S(1)} %join.8), channel_id=1, source_target_pairs={{0,24},{1,7},{2,26},{3,1},{4,28},{5,3},{6,30},{7,5},{8,0},{9,15},{... | collective-permute-start | bytes 2211848 | tf_op jit(solution)/shard_map/ppermute | solution.py:32
  87.9 16.0 %collective-permute-start = (bf16[16,48,624]{2,1,0:T(8,128)(2,1)S(1)}, bf16[16,48,624]{2,1,0:T(8,128)(2,1)S(1)}, u32[]{:S(2)}, u32[]{:S(2)}) collective-permute-start(bf16[16,48,624]{2,1,0:T(8,128)(2,1)S(1)} %all_to_all.5.refs_0_), channel_id=1, source_target_pairs={{0,1},{1,0},{2,3},{3,2},{4,5},{5,4},{6,7},{7,6},{8,9},{9,8},{10,11... | collective-permute-start | bytes 2875400 | tf_op jit(solution)/shard_map/ppermute | solution.py:22
  98.5 48.5 %collective-permute-start.22 = (bf16[576,1280]{1,0:T(8,128)(2,1)S(1)}, bf16[576,1280]{1,0:T(8,128)(2,1)S(1)}, u32[]{:S(2)}, u32[]{:S(2)}) collective-permute-start(bf16[576,1280]{1,0:T(8,128)(2,1)S(1)} %join.9), channel_id=1, source_target_pairs={{0,2},{1,9},{2,4},{3,11},{4,6},{5,13},{6,0},{7,15},{8,10},{9,17},{... | collective-permute-start | bytes 4423688 | tf_op jit(solution)/shard_map/ppermute | solution.py:32
  102.3 44.8 %collective-permute-start.23 = (bf16[576,1280]{1,0:T(8,128)(2,1)S(1)}, bf16[576,1280]{1,0:T(8,128)(2,1)S(1)}, u32[]{:S(2)}, u32[]{:S(2)}) collective-permute-start(bf16[576,1280]{1,0:T(8,128)(2,1)S(1)} %join.9), channel_id=1, source_target_pairs={{0,6},{1,25},{2,0},{3,27},{4,2},{5,29},{6,4},{7,31},{8,14},{9,1},{... | collective-permute-start | bytes 4423688 | tf_op jit(solution)/shard_map/ppermute | solution.py:32
  102.3 21.2 %collective-permute-start.7 = (bf16[192,1280]{1,0:T(8,128)(2,1)S(1)}, bf16[192,1280]{1,0:T(8,128)(2,1)S(1)}, u32[]{:S(2)}, u32[]{:S(2)}) collective-permute-start(bf16[192,1280]{1,0:T(8,128)(2,1)S(1)} %slice.24), channel_id=1, source_target_pairs={{0,2},{1,9},{2,4},{3,11},{4,6},{5,13},{6,0},{7,15},{8,10},{9,17},{... | collective-permute-start | bytes 1474568 | tf_op jit(solution)/shard_map/ppermute | solution.py:32
  103.9 26.4 %collective-permute-start.8 = (bf16[192,1280]{1,0:T(8,128)(2,1)S(1)}, bf16[192,1280]{1,0:T(8,128)(2,1)S(1)}, u32[]{:S(2)}, u32[]{:S(2)}) collective-permute-start(bf16[192,1280]{1,0:T(8,128)(2,1)S(1)} %slice.25), channel_id=1, source_target_pairs={{0,6},{1,25},{2,0},{3,27},{4,2},{5,29},{6,4},{7,31},{8,14},{9,1},{... | collective-permute-start | bytes 1474568 | tf_op jit(solution)/shard_map/ppermute | solution.py:32
  123.5 11.8 %collective-permute-start.20 = (bf16[288,1280]{1,0:T(8,128)(2,1)S(1)}, bf16[288,1280]{1,0:T(8,128)(2,1)S(1)}, u32[]{:S(2)}, u32[]{:S(2)}) collective-permute-start(bf16[288,1280]{1,0:T(8,128)(2,1)S(1)} %join.8), channel_id=1, source_target_pairs={{0,2},{1,9},{2,4},{3,11},{4,6},{5,13},{6,0},{7,15},{8,10},{9,17},{... | collective-permute-start | bytes 2211848 | tf_op jit(solution)/shard_map/ppermute | solution.py:32
  130.2 16.8 %collective-permute-start.19 = (bf16[288,1280]{1,0:T(8,128)(2,1)S(1)}, bf16[288,1280]{1,0:T(8,128)(2,1)S(1)}, u32[]{:S(2)}, u32[]{:S(2)}) collective-permute-start(bf16[288,1280]{1,0:T(8,128)(2,1)S(1)} %collective-permute-done.17.refs_0_), channel_id=1, source_target_pairs={{0,8},{1,3},{2,10},{3,5},{4,12},{5,7},{6,14},{7,1},{8,16},{9,11},{... | collective-permute-start | bytes 2211848 | tf_op jit(solution)/shard_map/ppermute | solution.py:32
  135.3 23.0 %collective-permute-start.21 = (bf16[288,1280]{1,0:T(8,128)(2,1)S(1)}, bf16[288,1280]{1,0:T(8,128)(2,1)S(1)}, u32[]{:S(2)}, u32[]{:S(2)}) collective-permute-start(bf16[288,1280]{1,0:T(8,128)(2,1)S(1)} %join.8), channel_id=1, source_target_pairs={{0,6},{1,25},{2,0},{3,27},{4,2},{5,29},{6,4},{7,31},{8,14},{9,1},{... | collective-permute-start | bytes 2211848 | tf_op jit(solution)/shard_map/ppermute | solution.py:32
  147.0 20.0 %collective-permute-start.24 = (bf16[288,1280]{1,0:T(8,128)(2,1)S(1)}, bf16[288,1280]{1,0:T(8,128)(2,1)S(1)}, u32[]{:S(2)}, u32[]{:S(2)}) collective-permute-start(bf16[288,1280]{1,0:T(8,128)(2,1)S(1)} %collective-permute-done.20), channel_id=1, source_target_pairs={{0,2},{1,9},{2,4},{3,11},{4,6},{5,13},{6,0},{7,15},{8,10},{9,17},{... | collective-permute-start | bytes 2211848 | tf_op jit(solution)/shard_map/ppermute | solution.py:32
  147.0 26.1 %collective-permute-start.25 = (bf16[288,1280]{1,0:T(8,128)(2,1)S(1)}, bf16[288,1280]{1,0:T(8,128)(2,1)S(1)}, u32[]{:S(2)}, u32[]{:S(2)}) collective-permute-start(bf16[288,1280]{1,0:T(8,128)(2,1)S(1)} %collective-permute-done.19), channel_id=1, source_target_pairs={{0,2},{1,9},{2,4},{3,11},{4,6},{5,13},{6,0},{7,15},{8,10},{9,17},{... | collective-permute-start | bytes 2211848 | tf_op jit(solution)/shard_map/ppermute | solution.py:32
  147.0 14.1 %collective-permute-start.26 = (bf16[288,1280]{1,0:T(8,128)(2,1)S(1)}, bf16[288,1280]{1,0:T(8,128)(2,1)S(1)}, u32[]{:S(2)}, u32[]{:S(2)}) collective-permute-start(bf16[288,1280]{1,0:T(8,128)(2,1)S(1)} %collective-permute-done.19), channel_id=1, source_target_pairs={{0,6},{1,25},{2,0},{3,27},{4,2},{5,29},{6,4},{7,31},{8,14},{9,1},{... | collective-permute-start | bytes 2211848 | tf_op jit(solution)/shard_map/ppermute | solution.py:32
  149.9 27.2 %collective-permute-start.27 = (bf16[144,1280]{1,0:T(8,128)(2,1)S(1)}, bf16[144,1280]{1,0:T(8,128)(2,1)S(1)}, u32[]{:S(2)}, u32[]{:S(2)}) collective-permute-start(bf16[144,1280]{1,0:T(8,128)(2,1)S(1)} %slice.28), channel_id=1, source_target_pairs={{0,2},{1,9},{2,4},{3,11},{4,6},{5,13},{6,0},{7,15},{8,10},{9,17},{... | collective-permute-start | bytes 1105928 | tf_op jit(solution)/shard_map/ppermute | solution.py:32
  158.4 19.7 %collective-permute-start.28 = (bf16[432,1280]{1,0:T(8,128)(2,1)S(1)}, bf16[432,1280]{1,0:T(8,128)(2,1)S(1)}, u32[]{:S(2)}, u32[]{:S(2)}) collective-permute-start(bf16[432,1280]{1,0:T(8,128)(2,1)S(1)} %slice.29), channel_id=1, source_target_pairs={{0,6},{1,25},{2,0},{3,27},{4,2},{5,29},{6,4},{7,31},{8,14},{9,1},{... | collective-permute-start | bytes 3317768 | tf_op jit(solution)/shard_map/ppermute | solution.py:32
  161.1 20.3 %collective-permute-start.29 = (bf16[288,1280]{1,0:T(8,128)(2,1)S(1)}, bf16[288,1280]{1,0:T(8,128)(2,1)S(1)}, u32[]{:S(2)}, u32[]{:S(2)}) collective-permute-start(bf16[288,1280]{1,0:T(8,128)(2,1)S(1)} %collective-permute-done.26), channel_id=1, source_target_pairs={{0,6},{1,25},{2,0},{3,27},{4,2},{5,29},{6,4},{7,31},{8,14},{9,1},{... | collective-permute-start | bytes 2211848 | tf_op jit(solution)/shard_map/ppermute | solution.py:32
  182.6 24.1 %collective-permute-start.30 = (f32[312,1280]{1,0:T(8,128)S(1)}, f32[312,1280]{1,0:T(8,128)S(1)}, u32[]{:S(2)}, u32[]{:S(2)}) collective-permute-start(f32[312,1280]{1,0:T(8,128)S(1)} %get-tuple-element.54), channel_id=1, source_target_pairs={{0,1},{1,0},{2,3},{3,2},{4,5},{5,4},{6,7},{7,6},{8,9},{9,8},{10,11... | collective-permute-start | bytes 4792328 | tf_op jit(solution)/shard_map/ppermute | solution.py:22
  (1 other events, 0.7 us)

commit v3 on v2

--- a/solution.py
+++ b/solution.py
@@ -126,8 +126,7 @@
 
 
 def gathered_briefly(own):
-    before, after = along_plane(own, 0, 1), along_plane(own, 0, -1)
-    far = along_plane(before, 0, 1)
+    before, after, far = (along_plane(own, 0, step) for step in (1, -1, 2))
     line = join([own, before, after, far])
     left, right = along_plane(line, 1, 1), along_plane(line, 1, -1)
     cut = line.shape[0] // 2
@@ -249,7 +248,8 @@
         return lax.dot_general(weight, block, (((0,), (0,)), ((), ())), preferred_element_type=jnp.float32)
 
     (weight,) = arrange([[(u, v, dcore, dy) for u, v in offsets for dcore, dy in OWN]], rows, other_rows)
-    tile = product(weight, join(early))
+    early = join(early)
+    tile = product(weight, early)
     layout = []
     for offsets, skipped, block in parts:
         blocks = [(u, v, dcore, dy - 1) for u, v in offsets for dcore, dy in OTHERS]

time: 213 us -> 207 us (0.972); the launches traced: 209 us -> 206 us
    ppermute x4, starting transfers between devices: 36.2 us -> 29.2 us  [swap_cores(): return lax.ppermute(block, 'core', [(0, 1), (1, 0)])]
    ppermute x20, starting transfers between devices: 19 us -> 24.7 us  [along_plane(): return lax.ppermute(block, ('x', 'z', 'core'), route)]
    ppermute x20, waiting for transfers between devices: 59.5 us -> 56.3 us  [along_plane(): return lax.ppermute(block, ('x', 'z', 'core'), route)]
  transfers between devices with their start and end apart: 31 -> 31, of which waited for: 14 -> 13; matrix products, arithmetic and copies ran while one was open for 9% -> 10% of each run, Pallas kernels for 1% -> 1%
where the time goes in v3:
time: 207 us; the launch traced here: 206 us
  waiting for transfers between devices  93.8 us (45%)
  starting transfers between devices  61.1 us (30%)
  blocking collectives  23.5 us (11%)
  matrix products  17.1 us (8%)
  Pallas kernels  4.59 us (2%)
  other arithmetic  3.28 us (2%)
  local copies, waits for them, and re-layouts  2.1 us (1%)
    ppermute x20, waiting for transfers between devices, along_plane(): return lax.ppermute(block, ('x', 'z', 'core'), route)  56.3 us
    ppermute x7, waiting for transfers between devices, along_y(): lax.ppermute(block, 'y', [(i, (i + step) % SIDE) for i in range(SIDE)])  34.4 us
    ppermute x4, starting transfers between devices, swap_cores(): return lax.ppermute(block, 'core', [(0, 1), (1, 0)])  29.2 us
    ppermute x20, starting transfers between devices, along_plane(): return lax.ppermute(block, ('x', 'z', 'core'), route)  24.7 us
    all_to_all x1, blocking collectives, body(): rows = lax.all_to_all(rows, ('x', 'z'), 0, 0, tiled=True)  23.5 us
    dot_general x14, matrix products, product(): lax.dot_general(weight, block, (((0,), (0,)), ((), ())), preferred_elemen...  17.1 us
    ppermute x7, starting transfers between devices, along_y(): lax.ppermute(block, 'y', [(i, (i + step) % SIDE) for i in range(SIDE)])  7.07 us
  transfers between devices with their start and end apart: 31, of which 13 were waited for; matrix products, arithmetic and copies ran while one was open for 10% of the time, Pallas kernels for 1%

profile of v3, /device:TPU:1, one launch (start us, length us, event | category | flops | bytes accessed | tf_op | source)
XLA Modules:
  0.0 205.7 jit_solution(18426256909808356448)
XLA Ops:
  3.0 23.5 %all_to_all.5.refs_0_ = bf16[16,48,624]{2,1,0:T(8,128)(2,1)S(1)} all-to-all(bf16[16,48,624]{2,1,0:T(8,128)(2,1)S(1)} %get-tuple-element.30), channel_id=1, replica_groups=mesh['y'=4,'x'=4,'z'=4,'core'=2] {'x','z'}, dimensions={0} | all-to-all | bytes 1916928 | tf_op jit(solution)/shard_map/all_to_all | solution.py:236
  27.8 1.4 collective-permute-start.9
  29.2 2.3 %collective-permute-start.1 = (bf16[4,48,1280]{2,1,0:T(8,128)(2,1)S(1)}, bf16[4,48,1280]{2,1,0:T(8,128)(2,1)S(1)}, u32[]{:S(2)}, u32[]{:S(2)}) collective-permute-start(bf16[4,48,1280]{2,1,0:T(8,128)(2,1)S(1)} %get-tuple-element.35), channel_id=1, source_target_pairs={{0,1},{1,0},{2,3},{3,2},{4,5},{5,4},{6,7},{7,6},{8,9},{9,8},{10,11... | collective-permute-start | bytes 1474568 | tf_op jit(solution)/shard_map/ppermute | solution.py:22
  31.5 17.8 %collective-permute-done.10.refs_3_ = bf16[16,48,624]{2,1,0:T(8,128)(2,1)S(1)} collective-permute-done((bf16[16,48,624]{2,1,0:T(8,128)(2,1)S(1)}, bf16[16,48,624]{2,1,0:T(8,128)(2,1)S(1)}, u32[]{:S(2)}, u32[]{:S(2)}) %collective-permute-start.10) | collective-permute-done | bytes 958496 | tf_op jit(solution)/shard_map/ppermute | solution.py:18
  49.5 2.7 %collective-permute-start.12 = (bf16[8,48,624]{2,1,0:T(8,128)(2,1)S(1)}, bf16[8,48,624]{2,1,0:T(8,128)(2,1)S(1)}, u32[]{:S(2)}, u32[]{:S(2)}) collective-permute-start(bf16[8,48,624]{2,1,0:T(8,128)(2,1)S(1)} %slice.27), channel_id=1, source_target_pairs={{0,96},{32,0},{64,32},{96,64},{1,97},{33,1},{65,33},{97,65},{2,98}... | collective-permute-start | bytes 1437704 | tf_op jit(solution)/shard_map/ppermute | solution.py:18
  53.8 12.3 %collective-permute-done.14.refs_0_ = bf16[96,1280]{1,0:T(8,128)(2,1)S(1)} collective-permute-done((bf16[96,1280]{1,0:T(8,128)(2,1)S(1)}, bf16[96,1280]{1,0:T(8,128)(2,1)S(1)}, u32[]{:S(2)}, u32[]{:S(2)}) %collective-permute-start.14) | collective-permute-done | bytes 245792 | tf_op jit(solution)/shard_map/ppermute | solution.py:18
  66.1 4.3 %collective-permute-done.16.refs_2_ = bf16[96,1280]{1,0:T(8,128)(2,1)S(1)} collective-permute-done((bf16[96,1280]{1,0:T(8,128)(2,1)S(1)}, bf16[96,1280]{1,0:T(8,128)(2,1)S(1)}, u32[]{:S(2)}, u32[]{:S(2)}) %collective-permute-start.16) | collective-permute-done | bytes 245792 | tf_op jit(solution)/shard_map/ppermute | solution.py:18
  70.5 2.5 %collective-permute-start.17 = (bf16[288,1280]{1,0:T(8,128)(2,1)S(1)}, bf16[288,1280]{1,0:T(8,128)(2,1)S(1)}, u32[]{:S(2)}, u32[]{:S(2)}) collective-permute-start(bf16[288,1280]{1,0:T(8,128)(2,1)S(1)} %join.8), channel_id=1, source_target_pairs={{0,8},{1,3},{2,10},{3,5},{4,12},{5,7},{6,14},{7,1},{8,16},{9,11},{... | collective-permute-start | bytes 2211848 | tf_op jit(solution)/shard_map/ppermute | solution.py:32
  73.3 2.0 collective-permute-start.13
  76.3 1.6 collective-permute-start.3
  78.2 9.5 %collective-permute-done.2.refs_1_ = bf16[96,1280]{1,0:T(8,128)(2,1)S(1)} collective-permute-done((bf16[96,1280]{1,0:T(8,128)(2,1)S(1)}, bf16[96,1280]{1,0:T(8,128)(2,1)S(1)}, u32[]{:S(2)}, u32[]{:S(2)}) %collective-permute-start.2) | collective-permute-done | bytes 245792 | tf_op jit(solution)/shard_map/ppermute | solution.py:32
  87.8 2.7 %collective-permute-start.6 = (bf16[384,1280]{1,0:T(8,128)(2,1)S(1)}, bf16[384,1280]{1,0:T(8,128)(2,1)S(1)}, u32[]{:S(2)}, u32[]{:S(2)}) collective-permute-start(bf16[384,1280]{1,0:T(8,128)(2,1)S(1)} %join.5.refs_0_), channel_id=1, source_target_pairs={{0,6},{1,25},{2,0},{3,27},{4,2},{5,29},{6,4},{7,31},{8,14},{9,1},{... | collective-permute-start | bytes 2949128 | tf_op jit(solution)/shard_map/ppermute | solution.py:32
  90.5 6.5 %collective-permute-start = (bf16[16,48,624]{2,1,0:T(8,128)(2,1)S(1)}, bf16[16,48,624]{2,1,0:T(8,128)(2,1)S(1)}, u32[]{:S(2)}, u32[]{:S(2)}) collective-permute-start(bf16[16,48,624]{2,1,0:T(8,128)(2,1)S(1)} %all_to_all.5.refs_0_), channel_id=1, source_target_pairs={{0,1},{1,0},{2,3},{3,2},{4,5},{5,4},{6,7},{7,6},{8,9},{9,8},{10,11... | collective-permute-start | bytes 2875400 | tf_op jit(solution)/shard_map/ppermute | solution.py:22
  97.0 6.2 %collective-permute-done.18.refs_1_ = bf16[288,1280]{1,0:T(8,128)(2,1)S(1)} collective-permute-done((bf16[288,1280]{1,0:T(8,128)(2,1)S(1)}, bf16[288,1280]{1,0:T(8,128)(2,1)S(1)}, u32[]{:S(2)}, u32[]{:S(2)}) %collective-permute-start.18) | collective-permute-done | bytes 737312 | tf_op jit(solution)/shard_map/ppermute | solution.py:32
  103.2 3.2 %collective-permute-start.22 = (bf16[576,1280]{1,0:T(8,128)(2,1)S(1)}, bf16[576,1280]{1,0:T(8,128)(2,1)S(1)}, u32[]{:S(2)}, u32[]{:S(2)}) collective-permute-start(bf16[576,1280]{1,0:T(8,128)(2,1)S(1)} %join.9), channel_id=1, source_target_pairs={{0,2},{1,9},{2,4},{3,11},{4,6},{5,13},{6,0},{7,15},{8,10},{9,17},{... | collective-permute-start | bytes 4423688 | tf_op jit(solution)/shard_map/ppermute | solution.py:32
  106.5 1.5 collective-permute-start.7
  109.4 18.9 %collective-permute-done.7.refs_3_ = bf16[192,1280]{1,0:T(8,128)(2,1)S(1)} collective-permute-done((bf16[192,1280]{1,0:T(8,128)(2,1)S(1)}, bf16[192,1280]{1,0:T(8,128)(2,1)S(1)}, u32[]{:S(2)}, u32[]{:S(2)}) %collective-permute-start.7) | collective-permute-done | bytes 491552 | tf_op jit(solution)/shard_map/ppermute | solution.py:32
  128.3 2.0 collective-permute-start.20
  130.5 1.8 collective-permute-start.19
  132.7 7.4 %collective-permute-done.20 = bf16[288,1280]{1,0:T(8,128)(2,1)S(1)} collective-permute-done((bf16[288,1280]{1,0:T(8,128)(2,1)S(1)}, bf16[288,1280]{1,0:T(8,128)(2,1)S(1)}, u32[]{:S(2)}, u32[]{:S(2)}) %collective-permute-start.20) | collective-permute-done | bytes 737312 | tf_op jit(solution)/shard_map/ppermute | solution.py:32
  140.1 5.4 %collective-permute-done.19 = bf16[288,1280]{1,0:T(8,128)(2,1)S(1)} collective-permute-done((bf16[288,1280]{1,0:T(8,128)(2,1)S(1)}, bf16[288,1280]{1,0:T(8,128)(2,1)S(1)}, u32[]{:S(2)}, u32[]{:S(2)}) %collective-permute-start.19) | collective-permute-done | bytes 737312 | tf_op jit(solution)/shard_map/ppermute | solution.py:32
  145.5 2.1 %collective-permute-start.25 = (bf16[288,1280]{1,0:T(8,128)(2,1)S(1)}, bf16[288,1280]{1,0:T(8,128)(2,1)S(1)}, u32[]{:S(2)}, u32[]{:S(2)}) collective-permute-start(bf16[288,1280]{1,0:T(8,128)(2,1)S(1)} %collective-permute-done.19), channel_id=1, source_target_pairs={{0,2},{1,9},{2,4},{3,11},{4,6},{5,13},{6,0},{7,15},{8,10},{9,17},{... | collective-permute-start | bytes 2211848 | tf_op jit(solution)/shard_map/ppermute | solution.py:32
  151.7 2.8 %convolution_add_fusion.4 = f32[624,1280]{1,0:T(8,128)S(1)} fusion(f32[624,1280]{1,0:T(8,128)S(1)} %fusion, bf16[1536,624]{1,0:T(8,128)(2,1)S(1)} %arrange.2, bf16[1536,1280]{1,0:T(8,128)(2,1)S(1)} %join.6), kind=kOutput, calls=%fused_computation.4 | convolution fusion | flops 2454466560 | bytes 12238848 | tf_op jit(solution)/shard_map/dot_general | solution.py:248
  154.6 1.4 fusion.1
  158.5 1.9 collective-permute-start.28
  162.5 1.4 fusion.4
  164.4 1.4 fusion.5
  167.3 3.0 %collective-permute-done.25 = bf16[288,1280]{1,0:T(8,128)(2,1)S(1)} collective-permute-done((bf16[288,1280]{1,0:T(8,128)(2,1)S(1)}, bf16[288,1280]{1,0:T(8,128)(2,1)S(1)}, u32[]{:S(2)}, u32[]{:S(2)}) %collective-permute-start.25) | collective-permute-done | bytes 737312 | tf_op jit(solution)/shard_map/ppermute | solution.py:32
  176.8 4.2 %collective-permute-done.29 = bf16[288,1280]{1,0:T(8,128)(2,1)S(1)} collective-permute-done((bf16[288,1280]{1,0:T(8,128)(2,1)S(1)}, bf16[288,1280]{1,0:T(8,128)(2,1)S(1)}, u32[]{:S(2)}, u32[]{:S(2)}) %collective-permute-start.29) | collective-permute-done | bytes 737312 | tf_op jit(solution)/shard_map/ppermute | solution.py:32
  182.3 18.4 %collective-permute-start.30 = (f32[312,1280]{1,0:T(8,128)S(1)}, f32[312,1280]{1,0:T(8,128)S(1)}, u32[]{:S(2)}, u32[]{:S(2)}) collective-permute-start(f32[312,1280]{1,0:T(8,128)S(1)} %get-tuple-element.54), channel_id=1, source_target_pairs={{0,1},{1,0},{2,3},{3,2},{4,5},{5,4},{6,7},{7,6},{8,9},{9,8},{10,11... | collective-permute-start | bytes 4792328 | tf_op jit(solution)/shard_map/ppermute | solution.py:22
  200.7 3.1 %collective-permute-done.30.got_ref = f32[312,1280]{1,0:T(8,128)S(1)} collective-permute-done((f32[312,1280]{1,0:T(8,128)S(1)}, f32[312,1280]{1,0:T(8,128)S(1)}, u32[]{:S(2)}, u32[]{:S(2)}) %collective-permute-start.30) | collective-permute-done | bytes 1597472 | tf_op jit(solution)/shard_map/ppermute | solution.py:22
  203.8 1.9 assemble.1
  (74 shorter events, 28.1 us)
Async XLA Ops:
  0.0 1.2 copy-start
  26.5 22.8 %collective-permute-start.10 = (bf16[16,48,624]{2,1,0:T(8,128)(2,1)S(1)}, bf16[16,48,624]{2,1,0:T(8,128)(2,1)S(1)}, u32[]{:S(2)}, u32[]{:S(2)}) collective-permute-start(bf16[16,48,624]{2,1,0:T(8,128)(2,1)S(1)} %all_to_all.5.refs_0_), channel_id=1, source_target_pairs={{0,32},{32,64},{64,96},{96,0},{1,33},{33,65},{65,97},{97,1},{2,34}... | collective-permute-start | bytes 2875400 | tf_op jit(solution)/shard_map/ppermute | solution.py:18
  27.8 21.7 %collective-permute-start.9 = (bf16[16,48,624]{2,1,0:T(8,128)(2,1)S(1)}, bf16[16,48,624]{2,1,0:T(8,128)(2,1)S(1)}, u32[]{:S(2)}, u32[]{:S(2)}) collective-permute-start(bf16[16,48,624]{2,1,0:T(8,128)(2,1)S(1)} %all_to_all.5.refs_0_), channel_id=1, source_target_pairs={{0,96},{32,0},{64,32},{96,64},{1,97},{33,1},{65,33},{97,65},{2,98}... | collective-permute-start | bytes 2875400 | tf_op jit(solution)/shard_map/ppermute | solution.py:18
  29.2 23.0 %collective-permute-start.1 = (bf16[4,48,1280]{2,1,0:T(8,128)(2,1)S(1)}, bf16[4,48,1280]{2,1,0:T(8,128)(2,1)S(1)}, u32[]{:S(2)}, u32[]{:S(2)}) collective-permute-start(bf16[4,48,1280]{2,1,0:T(8,128)(2,1)S(1)} %get-tuple-element.35), channel_id=1, source_target_pairs={{0,1},{1,0},{2,3},{3,2},{4,5},{5,4},{6,7},{7,6},{8,9},{9,8},{10,11... | collective-permute-start | bytes 1474568 | tf_op jit(solution)/shard_map/ppermute | solution.py:22
  49.3 23.7 %collective-permute-start.11 = (bf16[8,48,624]{2,1,0:T(8,128)(2,1)S(1)}, bf16[8,48,624]{2,1,0:T(8,128)(2,1)S(1)}, u32[]{:S(2)}, u32[]{:S(2)}) collective-permute-start(bf16[8,48,624]{2,1,0:T(8,128)(2,1)S(1)} %slice.26), channel_id=1, source_target_pairs={{0,32},{32,64},{64,96},{96,0},{1,33},{33,65},{65,97},{97,1},{2,34}... | collective-permute-start | bytes 1437704 | tf_op jit(solution)/shard_map/ppermute | solution.py:18
  49.5 23.5 %collective-permute-start.12 = (bf16[8,48,624]{2,1,0:T(8,128)(2,1)S(1)}, bf16[8,48,624]{2,1,0:T(8,128)(2,1)S(1)}, u32[]{:S(2)}, u32[]{:S(2)}) collective-permute-start(bf16[8,48,624]{2,1,0:T(8,128)(2,1)S(1)} %slice.27), channel_id=1, source_target_pairs={{0,96},{32,0},{64,32},{96,64},{1,97},{33,1},{65,33},{97,65},{2,98}... | collective-permute-start | bytes 1437704 | tf_op jit(solution)/shard_map/ppermute | solution.py:18
  52.3 13.8 %collective-permute-start.14 = (bf16[96,1280]{1,0:T(8,128)(2,1)S(1)}, bf16[96,1280]{1,0:T(8,128)(2,1)S(1)}, u32[]{:S(2)}, u32[]{:S(2)}) collective-permute-start(bf16[96,1280]{1,0:T(8,128)(2,1)S(1)} %get-tuple-element.38), channel_id=1, source_target_pairs={{0,96},{32,0},{64,32},{96,64},{1,97},{33,1},{65,33},{97,65},{2,98}... | collective-permute-start | bytes 737288 | tf_op jit(solution)/shard_map/ppermute | solution.py:18
  52.5 13.6 %collective-permute-start.15 = (bf16[96,1280]{1,0:T(8,128)(2,1)S(1)}, bf16[96,1280]{1,0:T(8,128)(2,1)S(1)}, u32[]{:S(2)}, u32[]{:S(2)}) collective-permute-start(bf16[96,1280]{1,0:T(8,128)(2,1)S(1)} %get-tuple-element.39), channel_id=1, source_target_pairs={{0,64},{32,96},{64,0},{96,32},{1,65},{33,97},{65,1},{97,33},{2,66}... | collective-permute-start | bytes 737288 | tf_op jit(solution)/shard_map/ppermute | solution.py:18
  52.9 17.5 %collective-permute-start.16 = (bf16[96,1280]{1,0:T(8,128)(2,1)S(1)}, bf16[96,1280]{1,0:T(8,128)(2,1)S(1)}, u32[]{:S(2)}, u32[]{:S(2)}) collective-permute-start(bf16[96,1280]{1,0:T(8,128)(2,1)S(1)} %get-tuple-element.40), channel_id=1, source_target_pairs={{0,32},{32,64},{64,96},{96,0},{1,33},{33,65},{65,97},{97,1},{2,34}... | collective-permute-start | bytes 737288 | tf_op jit(solution)/shard_map/ppermute | solution.py:18
  70.5 20.0 %collective-permute-start.17 = (bf16[288,1280]{1,0:T(8,128)(2,1)S(1)}, bf16[288,1280]{1,0:T(8,128)(2,1)S(1)}, u32[]{:S(2)}, u32[]{:S(2)}) collective-permute-start(bf16[288,1280]{1,0:T(8,128)(2,1)S(1)} %join.8), channel_id=1, source_target_pairs={{0,8},{1,3},{2,10},{3,5},{4,12},{5,7},{6,14},{7,1},{8,16},{9,11},{... | collective-permute-start | bytes 2211848 | tf_op jit(solution)/shard_map/ppermute | solution.py:32
  73.3 75.9 %collective-permute-start.13 = (bf16[48,48,624]{2,1,0:T(8,128)(2,1)S(1)}, bf16[48,48,624]{2,1,0:T(8,128)(2,1)S(1)}, u32[]{:S(2)}, u32[]{:S(2)}) collective-permute-start(bf16[48,48,624]{2,1,0:T(8,128)(2,1)S(1)} %join.7.refs_0_), channel_id=1, source_target_pairs={{0,1},{1,0},{2,3},{3,2},{4,5},{5,4},{6,7},{7,6},{8,9},{9,8},{10,11... | collective-permute-start | bytes 8626184 | tf_op jit(solution)/shard_map/ppermute | solution.py:22
  75.3 12.4 %collective-permute-start.2 = (bf16[96,1280]{1,0:T(8,128)(2,1)S(1)}, bf16[96,1280]{1,0:T(8,128)(2,1)S(1)}, u32[]{:S(2)}, u32[]{:S(2)}) collective-permute-start(bf16[96,1280]{1,0:T(8,128)(2,1)S(1)} %get-tuple-element.36.refs_0_), channel_id=1, source_target_pairs={{0,8},{1,3},{2,10},{3,5},{4,12},{5,7},{6,14},{7,1},{8,16},{9,11},{... | collective-permute-start | bytes 737288 | tf_op jit(solution)/shard_map/ppermute | solution.py:32
  76.3 11.4 %collective-permute-start.3 = (bf16[96,1280]{1,0:T(8,128)(2,1)S(1)}, bf16[96,1280]{1,0:T(8,128)(2,1)S(1)}, u32[]{:S(2)}, u32[]{:S(2)}) collective-permute-start(bf16[96,1280]{1,0:T(8,128)(2,1)S(1)} %get-tuple-element.36.refs_0_), channel_id=1, source_target_pairs={{0,24},{1,7},{2,26},{3,1},{4,28},{5,3},{6,30},{7,5},{8,0},{9,15},{... | collective-permute-start | bytes 737288 | tf_op jit(solution)/shard_map/ppermute | solution.py:32
  77.9 9.7 %collective-permute-start.4 = (bf16[96,1280]{1,0:T(8,128)(2,1)S(1)}, bf16[96,1280]{1,0:T(8,128)(2,1)S(1)}, u32[]{:S(2)}, u32[]{:S(2)}) collective-permute-start(bf16[96,1280]{1,0:T(8,128)(2,1)S(1)} %get-tuple-element.36.refs_0_), channel_id=1, source_target_pairs={{0,16},{1,5},{2,18},{3,7},{4,20},{5,1},{6,22},{7,3},{8,24},{9,13},... | collective-permute-start | bytes 737288 | tf_op jit(solution)/shard_map/ppermute | solution.py:32
  87.8 18.7 %collective-permute-start.5 = (bf16[384,1280]{1,0:T(8,128)(2,1)S(1)}, bf16[384,1280]{1,0:T(8,128)(2,1)S(1)}, u32[]{:S(2)}, u32[]{:S(2)}) collective-permute-start(bf16[384,1280]{1,0:T(8,128)(2,1)S(1)} %join.5.refs_0_), channel_id=1, source_target_pairs={{0,2},{1,9},{2,4},{3,11},{4,6},{5,13},{6,0},{7,15},{8,10},{9,17},{... | collective-permute-start | bytes 2949128 | tf_op jit(solution)/shard_map/ppermute | solution.py:32
  87.8 18.7 %collective-permute-start.6 = (bf16[384,1280]{1,0:T(8,128)(2,1)S(1)}, bf16[384,1280]{1,0:T(8,128)(2,1)S(1)}, u32[]{:S(2)}, u32[]{:S(2)}) collective-permute-start(bf16[384,1280]{1,0:T(8,128)(2,1)S(1)} %join.5.refs_0_), channel_id=1, source_target_pairs={{0,6},{1,25},{2,0},{3,27},{4,2},{5,29},{6,4},{7,31},{8,14},{9,1},{... | collective-permute-start | bytes 2949128 | tf_op jit(solution)/shard_map/ppermute | solution.py:32
  90.5 12.6 %collective-permute-start.18 = (bf16[288,1280]{1,0:T(8,128)(2,1)S(1)}, bf16[288,1280]{1,0:T(8,128)(2,1)S(1)}, u32[]{:S(2)}, u32[]{:S(2)}) collective-permute-start(bf16[288,1280]{1,0:T(8,128)(2,1)S(1)} %join.8), channel_id=1, source_target_pairs={{0,24},{1,7},{2,26},{3,1},{4,28},{5,3},{6,30},{7,5},{8,0},{9,15},{... | collective-permute-start | bytes 2211848 | tf_op jit(solution)/shard_map/ppermute | solution.py:32
  90.5 17.6 %collective-permute-start = (bf16[16,48,624]{2,1,0:T(8,128)(2,1)S(1)}, bf16[16,48,624]{2,1,0:T(8,128)(2,1)S(1)}, u32[]{:S(2)}, u32[]{:S(2)}) collective-permute-start(bf16[16,48,624]{2,1,0:T(8,128)(2,1)S(1)} %all_to_all.5.refs_0_), channel_id=1, source_target_pairs={{0,1},{1,0},{2,3},{3,2},{4,5},{5,4},{6,7},{7,6},{8,9},{9,8},{10,11... | collective-permute-start | bytes 2875400 | tf_op jit(solution)/shard_map/ppermute | solution.py:22
  103.2 42.3 %collective-permute-start.22 = (bf16[576,1280]{1,0:T(8,128)(2,1)S(1)}, bf16[576,1280]{1,0:T(8,128)(2,1)S(1)}, u32[]{:S(2)}, u32[]{:S(2)}) collective-permute-start(bf16[576,1280]{1,0:T(8,128)(2,1)S(1)} %join.9), channel_id=1, source_target_pairs={{0,2},{1,9},{2,4},{3,11},{4,6},{5,13},{6,0},{7,15},{8,10},{9,17},{... | collective-permute-start | bytes 4423688 | tf_op jit(solution)/shard_map/ppermute | solution.py:32
  106.5 41.1 %collective-permute-start.23 = (bf16[576,1280]{1,0:T(8,128)(2,1)S(1)}, bf16[576,1280]{1,0:T(8,128)(2,1)S(1)}, u32[]{:S(2)}, u32[]{:S(2)}) collective-permute-start(bf16[576,1280]{1,0:T(8,128)(2,1)S(1)} %join.9), channel_id=1, source_target_pairs={{0,6},{1,25},{2,0},{3,27},{4,2},{5,29},{6,4},{7,31},{8,14},{9,1},{... | collective-permute-start | bytes 4423688 | tf_op jit(solution)/shard_map/ppermute | solution.py:32
  106.5 21.8 %collective-permute-start.7 = (bf16[192,1280]{1,0:T(8,128)(2,1)S(1)}, bf16[192,1280]{1,0:T(8,128)(2,1)S(1)}, u32[]{:S(2)}, u32[]{:S(2)}) collective-permute-start(bf16[192,1280]{1,0:T(8,128)(2,1)S(1)} %slice.24), channel_id=1, source_target_pairs={{0,2},{1,9},{2,4},{3,11},{4,6},{5,13},{6,0},{7,15},{8,10},{9,17},{... | collective-permute-start | bytes 1474568 | tf_op jit(solution)/shard_map/ppermute | solution.py:32
  108.1 22.4 %collective-permute-start.8 = (bf16[192,1280]{1,0:T(8,128)(2,1)S(1)}, bf16[192,1280]{1,0:T(8,128)(2,1)S(1)}, u32[]{:S(2)}, u32[]{:S(2)}) collective-permute-start(bf16[192,1280]{1,0:T(8,128)(2,1)S(1)} %slice.25), channel_id=1, source_target_pairs={{0,6},{1,25},{2,0},{3,27},{4,2},{5,29},{6,4},{7,31},{8,14},{9,1},{... | collective-permute-start | bytes 1474568 | tf_op jit(solution)/shard_map/ppermute | solution.py:32
  128.3 11.8 %collective-permute-start.20 = (bf16[288,1280]{1,0:T(8,128)(2,1)S(1)}, bf16[288,1280]{1,0:T(8,128)(2,1)S(1)}, u32[]{:S(2)}, u32[]{:S(2)}) collective-permute-start(bf16[288,1280]{1,0:T(8,128)(2,1)S(1)} %join.8), channel_id=1, source_target_pairs={{0,2},{1,9},{2,4},{3,11},{4,6},{5,13},{6,0},{7,15},{8,10},{9,17},{... | collective-permute-start | bytes 2211848 | tf_op jit(solution)/shard_map/ppermute | solution.py:32
  130.5 15.0 %collective-permute-start.19 = (bf16[288,1280]{1,0:T(8,128)(2,1)S(1)}, bf16[288,1280]{1,0:T(8,128)(2,1)S(1)}, u32[]{:S(2)}, u32[]{:S(2)}) collective-permute-start(bf16[288,1280]{1,0:T(8,128)(2,1)S(1)} %collective-permute-done.17.refs_0_), channel_id=1, source_target_pairs={{0,8},{1,3},{2,10},{3,5},{4,12},{5,7},{6,14},{7,1},{8,16},{9,11},{... | collective-permute-start | bytes 2211848 | tf_op jit(solution)/shard_map/ppermute | solution.py:32
  140.1 18.3 %collective-permute-start.21 = (bf16[288,1280]{1,0:T(8,128)(2,1)S(1)}, bf16[288,1280]{1,0:T(8,128)(2,1)S(1)}, u32[]{:S(2)}, u32[]{:S(2)}) collective-permute-start(bf16[288,1280]{1,0:T(8,128)(2,1)S(1)} %join.8), channel_id=1, source_target_pairs={{0,6},{1,25},{2,0},{3,27},{4,2},{5,29},{6,4},{7,31},{8,14},{9,1},{... | collective-permute-start | bytes 2211848 | tf_op jit(solution)/shard_map/ppermute | solution.py:32
  145.5 20.8 %collective-permute-start.24 = (bf16[288,1280]{1,0:T(8,128)(2,1)S(1)}, bf16[288,1280]{1,0:T(8,128)(2,1)S(1)}, u32[]{:S(2)}, u32[]{:S(2)}) collective-permute-start(bf16[288,1280]{1,0:T(8,128)(2,1)S(1)} %collective-permute-done.20), channel_id=1, source_target_pairs={{0,2},{1,9},{2,4},{3,11},{4,6},{5,13},{6,0},{7,15},{8,10},{9,17},{... | collective-permute-start | bytes 2211848 | tf_op jit(solution)/shard_map/ppermute | solution.py:32
  145.5 24.8 %collective-permute-start.25 = (bf16[288,1280]{1,0:T(8,128)(2,1)S(1)}, bf16[288,1280]{1,0:T(8,128)(2,1)S(1)}, u32[]{:S(2)}, u32[]{:S(2)}) collective-permute-start(bf16[288,1280]{1,0:T(8,128)(2,1)S(1)} %collective-permute-done.19), channel_id=1, source_target_pairs={{0,2},{1,9},{2,4},{3,11},{4,6},{5,13},{6,0},{7,15},{8,10},{9,17},{... | collective-permute-start | bytes 2211848 | tf_op jit(solution)/shard_map/ppermute | solution.py:32
  147.6 12.7 %collective-permute-start.26 = (bf16[288,1280]{1,0:T(8,128)(2,1)S(1)}, bf16[288,1280]{1,0:T(8,128)(2,1)S(1)}, u32[]{:S(2)}, u32[]{:S(2)}) collective-permute-start(bf16[288,1280]{1,0:T(8,128)(2,1)S(1)} %collective-permute-done.19), channel_id=1, source_target_pairs={{0,6},{1,25},{2,0},{3,27},{4,2},{5,29},{6,4},{7,31},{8,14},{9,1},{... | collective-permute-start | bytes 2211848 | tf_op jit(solution)/shard_map/ppermute | solution.py:32
  149.1 25.1 %collective-permute-start.27 = (bf16[144,1280]{1,0:T(8,128)(2,1)S(1)}, bf16[144,1280]{1,0:T(8,128)(2,1)S(1)}, u32[]{:S(2)}, u32[]{:S(2)}) collective-permute-start(bf16[144,1280]{1,0:T(8,128)(2,1)S(1)} %slice.28), channel_id=1, source_target_pairs={{0,2},{1,9},{2,4},{3,11},{4,6},{5,13},{6,0},{7,15},{8,10},{9,17},{... | collective-permute-start | bytes 1105928 | tf_op jit(solution)/shard_map/ppermute | solution.py:32
  158.5 16.8 %collective-permute-start.28 = (bf16[432,1280]{1,0:T(8,128)(2,1)S(1)}, bf16[432,1280]{1,0:T(8,128)(2,1)S(1)}, u32[]{:S(2)}, u32[]{:S(2)}) collective-permute-start(bf16[432,1280]{1,0:T(8,128)(2,1)S(1)} %slice.29), channel_id=1, source_target_pairs={{0,6},{1,25},{2,0},{3,27},{4,2},{5,29},{6,4},{7,31},{8,14},{9,1},{... | collective-permute-start | bytes 3317768 | tf_op jit(solution)/shard_map/ppermute | solution.py:32
  160.4 20.6 %collective-permute-start.29 = (bf16[288,1280]{1,0:T(8,128)(2,1)S(1)}, bf16[288,1280]{1,0:T(8,128)(2,1)S(1)}, u32[]{:S(2)}, u32[]{:S(2)}) collective-permute-start(bf16[288,1280]{1,0:T(8,128)(2,1)S(1)} %collective-permute-done.26), channel_id=1, source_target_pairs={{0,6},{1,25},{2,0},{3,27},{4,2},{5,29},{6,4},{7,31},{8,14},{9,1},{... | collective-permute-start | bytes 2211848 | tf_op jit(solution)/shard_map/ppermute | solution.py:32
  182.3 21.5 %collective-permute-start.30 = (f32[312,1280]{1,0:T(8,128)S(1)}, f32[312,1280]{1,0:T(8,128)S(1)}, u32[]{:S(2)}, u32[]{:S(2)}) collective-permute-start(f32[312,1280]{1,0:T(8,128)S(1)} %get-tuple-element.54), channel_id=1, source_target_pairs={{0,1},{1,0},{2,3},{3,2},{4,5},{5,4},{6,7},{7,6},{8,9},{9,8},{10,11... | collective-permute-start | bytes 4792328 | tf_op jit(solution)/shard_map/ppermute | solution.py:22
  (1 other events, 0.7 us)
